TPU v7x, 1024 devices: a whole 4x4x32 slice. The times are simulated.
1024 devices in a mesh: expert: 32 (over x, y, core), chan: 32 (over z).
Axes of the slice: x: 4, y: 4, z: 32, core: 2. Of those that a mesh axis runs over, the one named last changes fastest.
Arguments:
- tiles_in: bfloat16 [1024, 3, 3, 2048], P('expert', None, None, 'chan'), may hold values from -6 to 6
- grad_out: bfloat16 [1024, 3, 3, 2048], P('expert', None, None, 'chan'), may hold values from -6 to 6
- gate: bfloat16 [1024], P('expert'), may hold values from 0.19921875 to 1
- expert_id: int32 [1024, 1], P('expert'), may hold values from 0 to 31; in each aligned block of 32 rows (0 to 31, 32 to 63, ...) at most 2 rows name the same one
- w_conv: bfloat16 [32, 3, 3, 32, 16384], P('expert', None, None, None, 'chan'), may hold values from -0.375 to 0.375
- w_depth: bfloat16 [32, 9, 16384], P('expert', None, 'chan'), may hold values from -2 to 2
- w_out: bfloat16 [32, 16384, 2048], P('expert', 'chan'), may hold values from -0.046875 to 0.046875
Outputs:
- grad_input: bfloat16 [1024, 3, 3, 2048], P('expert', None, None, 'chan')
- grad_gate: bfloat16 [1024], P('expert')
Inputs may be any that keep to these rules, and one draw needn't show every extreme that they name: `expert_id`: within the 32 tiles of one index of expert, no expert is named more than 2 times, and in every draw some expert is named exactly 2 times there.
All inputs are finite; a program needn't handle non-finite values.
Results may differ from a plain program's by a relative error of at most 0.009.
Values may be sent and summed in bfloat16 or wider, within the bound.
No kernel may reach another device: no remote copies, remote signals or barrier semaphores. Data moves between devices by JAX's collectives and lax.ppermute only.
A program may use at most 32 MiB of HBM per device.

v0:
```python
import jax
import jax.numpy as jnp
from jax import lax
from jax.sharding import PartitionSpec as P

CAP = 2


def group_conv(field, kernel, count):
    return lax.conv_general_dilated(
        field,
        kernel,
        (1, 1),
        "SAME",
        dimension_numbers=("NHWC", "HWIO", "NHWC"),
        feature_group_count=count,
        preferred_element_type=jnp.float32,
    )


def conv_back(field, kernel, count, cotangent):
    forward_value, pullback = jax.vjp(lambda value: group_conv(value, kernel, count), field)
    return pullback(cotangent)[0]


def gelu_slope(value):
    normal_cdf = 0.5 * (1.0 + jax.scipy.special.erf(value * 0.7071067811865476))
    return normal_cdf + value * jnp.exp(-0.5 * value * value) * 0.3989422804014327


def depth_forward(field, taps):
    side = field.shape[1]
    padded = jnp.pad(field, ((0, 0), (1, 1), (1, 1), (0, 0))).astype(jnp.float32)
    total = jnp.zeros(field.shape, jnp.float32)
    for row_off in range(3):
        for col_off in range(3):
            total = total + padded[:, row_off : row_off + side, col_off : col_off + side, :] * taps[
                3 * row_off + col_off
            ].astype(jnp.float32)
    return total


def depth_back(field, taps):
    side = field.shape[1]
    padded = jnp.pad(field, ((0, 0), (1, 1), (1, 1), (0, 0))).astype(jnp.float32)
    total = jnp.zeros(field.shape, jnp.float32)
    for row_off in range(3):
        for col_off in range(3):
            total = total + padded[
                :, 2 - row_off : 2 - row_off + side, 2 - col_off : 2 - col_off + side, :
            ] * taps[3 * row_off + col_off].astype(jnp.float32)
    return total


def on_device(tiles_in, grad_out, gate, expert_id, w_conv, w_depth, w_out):
    owned, side = (tiles_in.shape[0], tiles_in.shape[1])
    local_feat = tiles_in.shape[3]
    sections = lax.axis_size("expert")
    capacity = CAP
    slots = sections * capacity
    chosen = expert_id[:, 0]
    matches = (chosen[:, None] == jnp.arange(sections, dtype=jnp.int32)[None, :]).astype(jnp.int32)
    rows_idx = jnp.arange(owned, dtype=jnp.int32)
    earlier = (rows_idx[:, None] > rows_idx[None, :]).astype(jnp.int32)
    before = jnp.dot(earlier, matches)
    rank = jnp.sum(before * matches, axis=1)
    slot = chosen * capacity + rank
    placing = (slot[:, None] == jnp.arange(slots, dtype=jnp.int32)[None, :]).astype(jnp.bfloat16)
    flat = jnp.concatenate([tiles_in.reshape(owned, -1), grad_out.reshape(owned, -1)], axis=1)
    outward = lax.dot_general(
        placing, flat, (((0,), (0,)), ((), ())), preferred_element_type=jnp.float32
    ).astype(jnp.bfloat16)
    gate_out = lax.dot_general(
        placing,
        gate.reshape(owned, 1),
        (((0,), (0,)), ((), ())),
        preferred_element_type=jnp.float32,
    ).astype(jnp.bfloat16)
    arrived, gate_in = (
        lax.all_to_all(
            outward.reshape(sections, capacity, -1),
            "expert",
            split_axis=0,
            concat_axis=0,
            tiled=True,
        ),
        lax.all_to_all(
            gate_out.reshape(sections, capacity), "expert", split_axis=0, concat_axis=0, tiled=True
        ),
    )
    width = side * side * local_feat
    arrived = arrived.reshape(slots, 2 * width)
    inputs = arrived[:, :width].reshape(slots, side, side, local_feat)
    grads = arrived[:, width:].reshape(slots, side, side, local_feat)
    gates = gate_in.reshape(slots).astype(jnp.float32)
    kernel = w_conv[0]
    taps = w_depth[0]
    project = w_out[0]
    hidden = project.shape[0]
    count = local_feat // kernel.shape[2]
    h_one = group_conv(inputs, kernel, count)
    active = jax.nn.gelu(h_one, approximate=False).astype(jnp.bfloat16)
    h_two = depth_forward(active, taps).astype(jnp.bfloat16)
    gathered = lax.all_gather(grads, "chan", axis=3, tiled=True)
    upper = lax.dot_general(
        gathered.reshape(slots * side * side, -1),
        project,
        (((1,), (1,)), ((), ())),
        preferred_element_type=jnp.float32,
    )
    upper = upper.reshape(slots, side, side, hidden)
    partial_grad = jnp.sum(h_two.astype(jnp.float32) * upper, axis=(1, 2, 3))
    gate_grad = lax.psum(partial_grad, "chan").astype(jnp.bfloat16)
    d_two = (gates[:, None, None, None] * upper).astype(jnp.bfloat16)
    d_act = depth_back(d_two, taps)
    d_one = (d_act * gelu_slope(h_one)).astype(jnp.bfloat16)
    d_input = conv_back(inputs, kernel, count, d_one.astype(jnp.float32))
    back_rows, back_gate = (
        lax.all_to_all(
            d_input.reshape(sections, capacity, -1),
            "expert",
            split_axis=0,
            concat_axis=0,
            tiled=True,
        ),
        lax.all_to_all(
            gate_grad.reshape(sections, capacity), "expert", split_axis=0, concat_axis=0, tiled=True
        ),
    )
    grad_input = jnp.dot(
        placing, back_rows.reshape(slots, -1), preferred_element_type=jnp.float32
    ).astype(jnp.bfloat16)
    grad_gate = jnp.dot(
        placing, back_gate.reshape(slots, 1), preferred_element_type=jnp.float32
    ).astype(jnp.bfloat16)
    return (grad_input.reshape(owned, side, side, local_feat), grad_gate.reshape(owned))


def solution(mesh):
    in_specs = (
        P("expert", None, None, "chan"),
        P("expert", None, None, "chan"),
        P("expert"),
        P("expert", None),
        P("expert", None, None, None, "chan"),
        P("expert", None, "chan"),
        P("expert", "chan", None),
    )
    out_specs = (P("expert", None, None, "chan"), P("expert"))
    return jax.shard_map(
        on_device, mesh=mesh, in_specs=in_specs, out_specs=out_specs, check_vma=False
    )
```

profile of v0, /device:TPU:1, one launch (start us, length us, event | category | flops | bytes accessed | tf_op | source)
XLA Modules:
  0.0 281.6 jit_solution(7005515606834808140)
XLA Ops:
  7.2 0.0 all-gather.2.cloned.1.call-start
  7.2 1.0 fusion.36
  8.2 0.7 fusion.50
  8.8 0.9 copy.34
  9.8 0.1 reshape.164
  9.9 0.9 copy.35
  10.9 0.1 reshape.165
  11.0 0.3 convolution_convert_fusion
  11.3 0.1 reshape.166
  11.4 24.7 %all_to_all.30 = bf16[32,2,1152]{2,1,0:T(2,128)(2,1)S(1)} all-to-all(bf16[32,2,1152]{2,1,0:T(2,128)(2,1)S(1)} %reshape.166), channel_id=1, replica_groups=mesh['expert'=32,'chan'=32] {'expert'}, dimensions={0} | all-to-all | bytes 294912 | tf_op jit(solution)/shard_map/all_to_all | solution.py:80
  36.0 0.1 reshape.167
  36.1 0.1 fusion.53
  36.2 0.1 copy.36
  36.4 0.8 copy.37
  37.2 0.0 all-gather.2.cloned.1.call-update
  37.2 0.2 fusion.37
  37.4 0.7 all_to_all.24
  38.1 3.9 %all-to-all-start = ((bf16[32,1,2]{2,1,0:T(2,128)(2,1)}), bf16[32,1,2]{2,1,0:T(2,128)(2,1)S(1)}, u32[]{:S(2)}, u32[]{:S(2)}) async-start(bf16[32,1,2]{2,1,0:T(2,128)(2,1)} %all_to_all.24), calls=%async_computation | async-start | bytes 32768 | tf_op jit(solution)/shard_map/all_to_all | solution.py:87
  42.0 0.1 squeeze.5
  42.2 0.7 rev.3
  42.9 6.1 %all-to-all-done = bf16[32,1,2]{2,1,0:T(2,128)(2,1)S(1)} async-done(((bf16[32,1,2]{2,1,0:T(2,128)(2,1)}), bf16[32,1,2]{2,1,0:T(2,128)(2,1)S(1)}, u32[]{:S(2)}, u32[]{:S(2)}) %all-to-all-start) | async-done | bytes 160 | tf_op jit(solution)/shard_map/all_to_all | solution.py:87
  49.0 0.1 convert_reduce_fusion
  49.1 0.1 reshape.175
  49.2 0.2 copy.39
  49.3 0.7 convolution_bitcast_fusion
  50.0 0.1 copy.49
  50.2 110.2 %all-gather.2.cloned.1.call-done = bf16[64,3,3,2048]{0,2,1,3:T(4,128)(2,1)} async-done(((bf16[64,3,3,64]{0,2,1,3:T(4,128)(2,1)}), bf16[64,3,3,2048]{0,2,1,3:T(4,128)(2,1)}) %all-gather.2.cloned.1.call-update) | async-done | bytes 2359312 | tf_op jit(solution)/shard_map/all_gather | solution.py:104
  160.4 5.4 %multiply_convert_fusion = (bf16[64,3,3,512]{3,0,2,1:T(8,128)(2,1)S(1)}, f32[64,3,3,512]{3,0,2,1:T(8,128)S(1)}) fusion(f32[64]{0:T(128)S(1)} %reshape.175, bf16[1,512,2048]{2,1,0:T(8,128)(2,1)S(1)} %copy-done, bf16[64,3,3,2048]{0,2,1,3:T(4,128)(2,1)} %all-gather.2.cloned.1.call-done), kind=kOutput, calls=%fused_computation.67 | convolution fusion | flops 1208549376 | bytes 6226176 | tf_op jit(solution)/shard_map/dot_general | solution.py:105
  165.8 0.4 pad_convert_fusion.1
  166.2 4.5 %fusion.11 = (bf16[64,3,3,512]{3,0,2,1:T(8,128)(2,1)S(1)}, bf16[64,3,3,512]{3,0,2,1:T(8,128)(2,1)}) fusion(f32[64,3,3,512]{3,0,2,1:T(8,128)S(1)} %bitcast.54, f32[512]{0:T(512)S(1)} %bitcast.75, f32[64,5,5,512]{3,0,2,1:T(8,128)S(1)} %pad_convert_fusion.1, f32[512]{0:T(512)S(1)} %bitcast.77, f32[512]{0:T(512)S(1)} %bitcast.63, f32[512]{0:T(512)S(1)} %bitcast.65, ...), kind=kLoop, calls=%fused_computation.17 | loop fusion | flops 27131904 | bytes 12994560 | tf_op jit(solution)/shard_map/convert_element_type | solution.py:102
  170.7 0.4 pad_convert_fusion
  171.1 0.8 multiply_reduce_fusion
  172.0 40.9 %psum.7 = bf16[64]{0:T(256)(128)(2,1)S(1)} all-reduce(f32[64]{0:T(128)S(1)} %multiply_reduce_fusion), channel_id=1, replica_groups=mesh['expert'=32,'chan'=32] {'chan'}, use_global_device_ids=true, to_apply=%region_2.3 | all-reduce | flops 64 | bytes 384 | tf_op jit(solution)/shard_map/psum | solution.py:113
  212.8 0.7 all_to_all.25
  213.6 41.5 %all-to-all-start.3 = ((bf16[32,1,2]{2,1,0:T(2,128)(2,1)}), bf16[32,1,2]{2,1,0:T(2,128)(2,1)S(1)}, u32[]{:S(2)}, u32[]{:S(2)}) async-start(bf16[32,1,2]{2,1,0:T(2,128)(2,1)} %all_to_all.25), calls=%async_computation.3 | async-start | bytes 32768 | tf_op jit(solution)/shard_map/all_to_all | solution.py:126
  255.1 1.7 convolution_convert_fusion.1
  256.8 0.2 copy.44
  257.0 0.9 convert_element_type.194
  257.9 4.1 %all-to-all-done.3 = bf16[32,1,2]{2,1,0:T(2,128)(2,1)S(1)} async-done(((bf16[32,1,2]{2,1,0:T(2,128)(2,1)}), bf16[32,1,2]{2,1,0:T(2,128)(2,1)S(1)}, u32[]{:S(2)}, u32[]{:S(2)}) %all-to-all-start.3) | async-done | bytes 160 | tf_op jit(solution)/shard_map/all_to_all | solution.py:126
  262.0 4.2 %all-to-all-start.2 = ((bf16[32,2,576]{2,1,0:T(2,128)(2,1)}), bf16[32,2,576]{2,1,0:T(2,128)(2,1)S(1)}, u32[]{:S(2)}, u32[]{:S(2)}) async-start(bf16[32,2,576]{2,1,0:T(2,128)(2,1)} %convert_element_type.194), calls=%async_computation.2 | async-start | bytes 163840 | tf_op jit(solution)/shard_map/all_to_all | solution.py:119
  266.2 0.1 reduce.1
  266.2 0.1 reshape.188
  266.3 0.7 fusion.38
  267.1 6.6 %all-to-all-done.2 = bf16[32,2,576]{2,1,0:T(2,128)(2,1)S(1)} async-done(((bf16[32,2,576]{2,1,0:T(2,128)(2,1)}), bf16[32,2,576]{2,1,0:T(2,128)(2,1)S(1)}, u32[]{:S(2)}, u32[]{:S(2)}) %all-to-all-start.2) | async-done | bytes 73760 | tf_op jit(solution)/shard_map/all_to_all | solution.py:119
  273.7 0.1 reshape.172
  273.8 0.2 convolution_convert_fusion.2
  274.0 0.1 reshape.173
  274.1 0.6 copy.46
  (14 shorter events, 0.1 us)
Async XLA Ops:
  7.2 153.2 %copy-start = (bf16[1,512,2048]{2,1,0:T(8,128)(2,1)S(1)}, bf16[1,512,2048]{2,1,0:T(8,128)(2,1)}, u32[]{:S(2)}) copy-start(bf16[1,512,2048]{2,1,0:T(8,128)(2,1)} %param.13) | copy-start | bytes 6291460
  7.2 153.2 %all-gather.2.cloned.1.call-start = ((), (), s32[]{:S(2)}) async-start(), calls=%async_computation.4 | async-start | bytes 6488064 | tf_op jit(solution)/shard_map/all_gather | solution.py:104
  10.8 26.4 %copy-start.5 = (bf16[32]{0:T(256)(128)(2,1)S(1)}, bf16[32]{0:T(256)(128)(2,1)}, u32[]{:S(2)}) copy-start(bf16[32]{0:T(256)(128)(2,1)} %param.9) | copy-start | bytes 196
  11.0 31.0 %copy-start.3 = (bf16[1,3,3,32,512]{4,3,2,1,0:T(8,128)(2,1)S(1)}, bf16[1,3,3,32,512]{4,3,2,1,0:T(8,128)(2,1)}, u32[]{:S(2)}) copy-start(bf16[1,3,3,32,512]{4,3,2,1,0:T(8,128)(2,1)} %param.11) | copy-start | bytes 884740
  36.1 6.1 %copy-start.4 = (bf16[1,9,512]{2,1,0:T(8,128)(2,1)S(1)}, bf16[1,9,512]{2,1,0:T(8,128)(2,1)}, u32[]{:S(2)}) copy-start(bf16[1,9,512]{2,1,0:T(8,128)(2,1)} %param.12) | copy-start | bytes 27652
  38.1 10.9 %all-to-all-start = ((bf16[32,1,2]{2,1,0:T(2,128)(2,1)}), bf16[32,1,2]{2,1,0:T(2,128)(2,1)S(1)}, u32[]{:S(2)}, u32[]{:S(2)}) async-start(bf16[32,1,2]{2,1,0:T(2,128)(2,1)} %all_to_all.24), calls=%async_computation | async-start | bytes 32768 | tf_op jit(solution)/shard_map/all_to_all | solution.py:87
  171.1 84.0 %copy-start.1 = (bf16[64,3,3,512]{3,0,2,1:T(8,128)(2,1)S(1)}, bf16[64,3,3,512]{3,0,2,1:T(8,128)(2,1)}, u32[]{:S(2)}) copy-start(bf16[64,3,3,512]{3,0,2,1:T(8,128)(2,1)} %get-tuple-element.11) | copy-start | bytes 1769476
  171.1 84.0 %copy-start.2 = (bf16[3,3,64,256]{3,2,1,0:T(8,128)(2,1)S(1)}, bf16[3,3,64,256]{3,2,1,0:T(8,128)(2,1)}, u32[]{:S(2)}) copy-start(bf16[3,3,64,256]{3,2,1,0:T(8,128)(2,1)} %rev.3) | copy-start | bytes 884740
  213.6 48.4 %all-to-all-start.3 = ((bf16[32,1,2]{2,1,0:T(2,128)(2,1)}), bf16[32,1,2]{2,1,0:T(2,128)(2,1)S(1)}, u32[]{:S(2)}, u32[]{:S(2)}) async-start(bf16[32,1,2]{2,1,0:T(2,128)(2,1)} %all_to_all.25), calls=%async_computation.3 | async-start | bytes 32768 | tf_op jit(solution)/shard_map/all_to_all | solution.py:126
  262.0 11.7 %all-to-all-start.2 = ((bf16[32,2,576]{2,1,0:T(2,128)(2,1)}), bf16[32,2,576]{2,1,0:T(2,128)(2,1)S(1)}, u32[]{:S(2)}, u32[]{:S(2)}) async-start(bf16[32,2,576]{2,1,0:T(2,128)(2,1)} %convert_element_type.194), calls=%async_computation.2 | async-start | bytes 163840 | tf_op jit(solution)/shard_map/all_to_all | solution.py:119
Sparse Core Ops, SparseCore 0:
  37.3 122.9 all-gather.1
where the time goes:
time: 282 us
  waiting for transfers between devices  127 us (45%)
  blocking collectives  65.5 us (23%)
  starting transfers between devices  49.6 us (18%)
  between operations  14.3 us (5%)
  matrix products  10.1 us (4%)
  local copies, waits for them, and re-layouts  8.07 us (3%)
  other arithmetic  6.92 us (2%)
    all_gather x1, waiting for transfers between devices, on_device(): gathered = lax.all_gather(grads, 'chan', axis=3, tiled=True)  110 us
    all_to_all x1, starting transfers between devices, on_device(): lax.all_to_all(gate_grad.reshape(sections, capacity), 'expert', split_axi...  41.5 us
    psum x1, blocking collectives, on_device(): gate_grad = lax.psum(partial_grad, 'chan').astype(jnp.bfloat16)  40.9 us
    all_to_all x1, blocking collectives, on_device(): lax.all_to_all(outward.reshape(sections, capacity, -1), 'expert', split_a...  24.7 us
    all_to_all x1, waiting for transfers between devices, on_device(): lax.all_to_all(d_input.reshape(sections, capacity, -1), 'expert', split_a...  6.64 us
    all_to_all x1, waiting for transfers between devices, on_device(): lax.all_to_all(gate_out.reshape(sections, capacity), 'expert', split_axis...  6.1 us
  transfers between devices with their start and end apart: 4, of which 4 were waited for; matrix products, arithmetic and copies ran while one was open for 2% of the time, Pallas kernels for 0%

commit v1 on v0

v1 whole, which is shorter than its diff:
```python
import jax
import jax.numpy as jnp
from jax import lax
from jax.experimental import pallas as pl
from jax.experimental.pallas import tpu as pltpu
from jax.sharding import PartitionSpec as P

CAP = 2


def near(pos, off, side):
    row, col = pos // side + off // 3 - 1, pos % side + off % 3 - 1
    return row * side + col if 0 <= row < side and 0 <= col < side else None


def project_kernel(feat_ref, weight_ref, h_two_ref, gate_ref, d_two_ref, part_ref, left_ref):
    blocks, rows, lanes = feat_ref.shape
    half = lanes // 2
    tokens, slots, hidden = d_two_ref.shape
    own = slots // 2
    for block in range(0, blocks, 2):
        first = feat_ref[block]
        second = feat_ref[block + 1]
        span = slice(block * half, (block + 2) * half)
        left_ref[:rows, span] = jnp.concatenate([first[:, :half], second[:, :half]], axis=1)
        left_ref[rows:, span] = jnp.concatenate([first[:, half:], second[:, half:]], axis=1)
    wide = 256
    for group in range(2):
        keep = slice(group * own, (group + 1) * own)
        scale = gate_ref[keep, :][:, :1]
        total = jnp.zeros((own, 128), jnp.float32)
        for start in range(0, hidden, wide):
            upper = lax.dot_general(
                left_ref[group * rows : (group + 1) * rows, :],
                weight_ref[start : start + wide, :],
                (((1,), (1,)), ((), ())),
                preferred_element_type=jnp.float32,
            )
            for pos in range(tokens):
                piece = upper[pos * own : (pos + 1) * own, :]
                d_two_ref[pos, keep, start : start + wide] = (piece * scale).astype(jnp.bfloat16)
                prod = h_two_ref[pos, keep, start : start + wide].astype(jnp.float32) * piece
                for lane in range(0, wide, 128):
                    total = total + prod[:, lane : lane + 128]
        part_ref[keep, :] = total


def back_kernel(d_two_ref, slope_ref, taps_ref, kernel_ref, d_in_ref, d_one_ref, *, side):
    tokens, slots, hidden = d_two_ref.shape
    wide = 256
    for start in range(0, hidden, wide):
        span = slice(start, start + wide)
        for pos in range(tokens):
            total = jnp.zeros((slots, wide), jnp.float32)
            for off in range(9):
                other = near(pos, 8 - off, side)
                if other is not None:
                    total = total + d_two_ref[other, :, span].astype(jnp.float32) * taps_ref[
                        off : off + 1, span
                    ].astype(jnp.float32)
            d_one_ref[pos, :, span] = (total * slope_ref[pos, :, span]).astype(jnp.bfloat16)
    for pos in range(tokens):
        total = jnp.zeros(d_in_ref.shape[1:], jnp.float32)
        for off in range(9):
            other = near(pos, 8 - off, side)
            if other is not None:
                total = total + lax.dot_general(
                    d_one_ref[other],
                    kernel_ref[off],
                    (((1,), (1,)), ((), ())),
                    preferred_element_type=jnp.float32,
                )
        d_in_ref[pos] = total.astype(jnp.bfloat16)


def vmem(count):
    return [pl.BlockSpec(memory_space=pltpu.VMEM) for _ in range(count)]


def forward(inputs, kernel, taps, side):
    tokens = side * side
    blank = jnp.zeros_like(inputs[0])
    columns = []
    for pos in range(tokens):
        picked = [near(pos, off, side) for off in range(9)]
        columns.append(
            jnp.concatenate([blank if n is None else inputs[n] for n in picked], axis=1)
        )
    h_one = jnp.einsum(
        "psk,kf->psf",
        jnp.stack(columns),
        kernel.reshape(-1, kernel.shape[2]),
        preferred_element_type=jnp.float32,
    )
    active = jax.nn.gelu(h_one, approximate=False).astype(jnp.bfloat16)
    grid = active.reshape(side, side, *active.shape[1:])
    padded = jnp.pad(grid, ((1, 1), (1, 1), (0, 0), (0, 0))).astype(jnp.float32)
    total = jnp.zeros(grid.shape, jnp.float32)
    for row in range(3):
        for col in range(3):
            total = total + padded[row : row + side, col : col + side] * taps[3 * row + col].astype(
                jnp.float32
            )
    h_two = total.reshape(active.shape).astype(jnp.bfloat16)
    cdf = 0.5 * (1.0 + lax.erf(h_one * 0.7071067811865476))
    slope = cdf + h_one * jnp.exp(-0.5 * h_one * h_one) * 0.3989422804014327
    return h_two, slope


def on_device(tiles_in, grad_out, gate, expert_id, w_conv, w_depth, w_out):
    owned, side, _, feat = tiles_in.shape
    tokens = side * side
    width = tokens * feat
    sections = lax.axis_size("expert")
    slots = sections * CAP
    hidden = w_out.shape[1]
    group = w_conv.shape[3]
    chosen = expert_id[:, 0]
    matches = (chosen[:, None] == jnp.arange(sections, dtype=jnp.int32)[None, :]).astype(jnp.int32)
    rows = jnp.arange(owned, dtype=jnp.int32)
    earlier = (rows[:, None] > rows[None, :]) & (chosen[:, None] == chosen[None, :])
    rank = jnp.sum(earlier.astype(jnp.int32), axis=1)
    slot = chosen * CAP + rank
    placing = (slot[:, None] == jnp.arange(slots, dtype=jnp.int32)[None, :]).astype(jnp.bfloat16)

    def place(array):
        out = lax.dot_general(
            placing, array, (((0,), (0,)), ((), ())), preferred_element_type=jnp.float32
        )
        return out.astype(jnp.bfloat16).reshape(sections, CAP, -1)

    def exchange(array):
        return lax.all_to_all(array, "expert", split_axis=0, concat_axis=0, tiled=True)

    tail = 64
    grads = exchange(place(grad_out.reshape(owned, width)))
    packed = grads.reshape(sections, CAP, tokens, feat).transpose(2, 0, 1, 3)
    packed = packed.reshape(tokens * sections, CAP * feat)
    extra = jnp.pad(gate[:, None], ((0, 0), (0, tail - 1)))
    outward = place(jnp.concatenate([tiles_in.reshape(owned, width), extra], axis=1))
    packed, outward = lax.optimization_barrier((packed, outward))
    gathered = lax.all_gather(packed, "chan", axis=0, tiled=False)
    arrived = exchange(outward)

    inputs = arrived[:, :, :width].reshape(sections, CAP, tokens, feat).transpose(2, 1, 0, 3)
    inputs = inputs.reshape(tokens, slots, feat)
    gates = arrived[:, :, width].T.reshape(slots, 1).astype(jnp.float32)
    gates = jnp.broadcast_to(gates, (slots, 128))
    taps = w_depth[0]
    small = w_conv[0].reshape(9, group, hidden)
    count = feat // group
    per = hidden // count
    which = jnp.arange(hidden, dtype=jnp.int32) // per
    kernel = jnp.concatenate(
        [jnp.where(which == g, small, jnp.zeros_like(small)) for g in range(count)], axis=1
    )
    h_two, slope = forward(inputs, kernel, taps, side)

    d_two, part = pl.pallas_call(
        project_kernel,
        out_shape=(
            jax.ShapeDtypeStruct((tokens, slots, hidden), jnp.bfloat16),
            jax.ShapeDtypeStruct((slots, 128), jnp.float32),
        ),
        in_specs=vmem(4),
        out_specs=tuple(vmem(2)),
        scratch_shapes=[
            pltpu.VMEM((tokens * slots, w_out.shape[2]), jnp.bfloat16),
        ],
        name="project",
    )(gathered, w_out[0], h_two, gates)
    part = jnp.sum(part, axis=1)
    part = jnp.pad(part, (0, 128 - slots))
    chans = lax.axis_size("chan")
    parts = lax.all_to_all(
        jnp.broadcast_to(part[None], (chans, 128)), "chan", split_axis=0, concat_axis=0, tiled=True
    )
    gate_grad = jnp.sum(parts, axis=0)[:slots].astype(jnp.bfloat16)
    d_input = pl.pallas_call(
        lambda *refs: back_kernel(*refs, side=side),
        out_shape=jax.ShapeDtypeStruct((tokens, slots, feat), jnp.bfloat16),
        in_specs=vmem(4),
        out_specs=vmem(1)[0],
        scratch_shapes=[pltpu.VMEM((tokens, slots, hidden), jnp.bfloat16)],
        name="back",
    )(d_two, slope, taps, kernel)
    d_input = d_input.reshape(tokens, CAP, sections, feat).transpose(2, 1, 0, 3)
    d_input = d_input.reshape(sections, CAP, width)
    extra = jnp.pad(gate_grad.reshape(CAP, sections).T[:, :, None], ((0, 0), (0, 0), (0, tail - 1)))
    back = exchange(jnp.concatenate([d_input, extra], axis=2))
    mine = jnp.dot(
        placing, back.reshape(slots, width + tail), preferred_element_type=jnp.float32
    ).astype(jnp.bfloat16)
    return (mine[:, :width].reshape(owned, side, side, feat), mine[:, width])


def solution(mesh):
    in_specs = (
        P("expert", None, None, "chan"),
        P("expert", None, None, "chan"),
        P("expert"),
        P("expert", None),
        P("expert", None, None, None, "chan"),
        P("expert", None, "chan"),
        P("expert", "chan", None),
    )
    out_specs = (P("expert", None, None, "chan"), P("expert"))
    return jax.shard_map(
        on_device, mesh=mesh, in_specs=in_specs, out_specs=out_specs, check_vma=False
    )
```

time: 282 us -> 236 us (0.84)
  blocking collectives: 65.5 us -> 37 us
  starting transfers between devices: 49.6 us -> 33.9 us
  Pallas kernels: 0 us -> 8.31 us
  waiting for transfers between devices: 127 us -> 121 us
  matrix products: 10.1 us -> 5.26 us
  local copies, waits for them, and re-layouts: 8.07 us -> 11.5 us
    psum x1 -> x0, blocking collectives: 40.9 us -> none  [on_device(): gate_grad = lax.psum(partial_grad, 'chan').astype(jnp.bfloat16)]
    all_gather x1, waiting for transfers between devices: 110 us -> 92.2 us  [on_device(): gathered = lax.all_gather(packed, 'chan', axis=0, tiled=False)]
    all_to_all x3, starting transfers between devices: 49.6 us -> 33.8 us  [the longest x2 21.5 us: exchange(): lax.all_to_all(array, 'expert', split_axis=0, concat_axis=0, tiled=True)]
    all_to_all x1, blocking collectives: 24.7 us -> 37 us  [exchange(): lax.all_to_all(array, 'expert', split_axis=0, concat_axis=0, tiled=True)]
    all_to_all x3, waiting for transfers between devices: 16.8 us -> 28.5 us  [the longest x1 16.4 us: on_device(): lax.all_to_all(jnp.broadcast_to(part[None], (chans, 128)), 'chan', split_...]
    pallas_call x0 -> x2, Pallas kernels: none -> 8.31 us  [the longest x1 4.72 us: on_device(): pl.pallas_call(project_kernel, out_shape=(jax.ShapeDtypeStruct((tokens, s...]
    convert_element_type x5 -> x4, other arithmetic: 5.35 us -> 1.94 us  [the longest x1 1.52 us: forward(): h_two = total.reshape(active.shape).astype(jnp.bfloat16)]
    dot_general x6 -> x4, matrix products: 7.78 us -> 5.26 us  [the longest x1 4.49 us: forward(): jnp.einsum('psk,kf->psf', jnp.stack(columns), kernel.reshape(-1, kernel.s...]
  transfers between devices with their start and end apart: 4 -> 4, of which waited for: 4 -> 4; matrix products, arithmetic and copies ran while one was open for 2% -> 5% of each run, Pallas kernels for 0% -> 2%
where the time goes in v1:
time: 236 us
  waiting for transfers between devices  121 us (51%)
  blocking collectives  37 us (16%)
  starting transfers between devices  33.9 us (14%)
  between operations  14.4 us (6%)
  local copies, waits for them, and re-layouts  11.5 us (5%)
  Pallas kernels  8.31 us (4%)
  matrix products  5.26 us (2%)
  other arithmetic  4.59 us (2%)
    all_gather x1, waiting for transfers between devices, on_device(): gathered = lax.all_gather(packed, 'chan', axis=0, tiled=False)  92.2 us
    all_to_all x1, blocking collectives, exchange(): lax.all_to_all(array, 'expert', split_axis=0, concat_axis=0, tiled=True)  37 us
    all_to_all x2, starting transfers between devices, exchange(): lax.all_to_all(array, 'expert', split_axis=0, concat_axis=0, tiled=True)  21.5 us
    all_to_all x1, waiting for transfers between devices, on_device(): lax.all_to_all(jnp.broadcast_to(part[None], (chans, 128)), 'chan', split_...  16.4 us
    all_to_all x1, starting transfers between devices, on_device(): lax.all_to_all(jnp.broadcast_to(part[None], (chans, 128)), 'chan', split_...  12.3 us
    all_to_all x2, waiting for transfers between devices, exchange(): lax.all_to_all(array, 'expert', split_axis=0, concat_axis=0, tiled=True)  12.2 us
    pallas_call x1, Pallas kernels, on_device(): pl.pallas_call(project_kernel, out_shape=(jax.ShapeDtypeStruct((tokens, s...  4.72 us
  transfers between devices with their start and end apart: 4, of which 4 were waited for; matrix products, arithmetic and copies ran while one was open for 5% of the time, Pallas kernels for 2%

profile of v1, /device:TPU:1, one launch (start us, length us, event | category | flops | bytes accessed | tf_op | source)
XLA Modules:
  0.0 235.7 jit_solution(14148894851581244640)
XLA Ops:
  7.2 0.9 convert_reduce_fusion
  8.1 0.7 fusion.41
  8.7 0.9 copy.91
  9.7 0.1 reshape.175
  9.8 0.3 convolution_convert_fusion.1
  10.1 0.7 reshape.176
  10.8 17.6 %all-to-all-start = ((bf16[32,2,576]{2,1,0:T(2,128)(2,1)}), bf16[32,2,576]{2,1,0:T(2,128)(2,1)S(1)}, u32[]{:S(2)}, u32[]{:S(2)}) async-start(bf16[32,2,576]{2,1,0:T(2,128)(2,1)} %reshape.176), calls=%async_computation | async-start | bytes 163840 | tf_op jit(solution)/shard_map/all_to_all | solution.py:133
  28.5 0.9 copy.94
  29.4 0.1 reshape.179
  29.5 0.8 copy.95
  30.3 0.3 convolution_convert_fusion
  30.6 0.7 reshape.180
  31.2 4.7 %all-to-all-done = bf16[32,2,576]{2,1,0:T(2,128)(2,1)S(1)} async-done(((bf16[32,2,576]{2,1,0:T(2,128)(2,1)}), bf16[32,2,576]{2,1,0:T(2,128)(2,1)S(1)}, u32[]{:S(2)}, u32[]{:S(2)}) %all-to-all-start) | async-done | bytes 73760 | tf_op jit(solution)/shard_map/all_to_all | solution.py:133
  36.0 0.2 reshape.177
  36.1 0.2 copy.93
  36.3 0.8 reshape.178
  37.2 3.9 %all-to-all-start.1 = ((bf16[32,2,640]{2,1,0:T(2,128)(2,1)}), bf16[32,2,640]{2,1,0:T(2,128)(2,1)S(1)}, u32[]{:S(2)}, u32[]{:S(2)}) async-start(bf16[32,2,640]{2,1,0:T(2,128)(2,1)} %reshape.180), calls=%async_computation.1 | async-start | bytes 163840 | tf_op jit(solution)/shard_map/all_to_all | solution.py:133
  41.1 7.5 %all-to-all-done.1 = bf16[32,2,640]{2,1,0:T(2,128)(2,1)S(1)} async-done(((bf16[32,2,640]{2,1,0:T(2,128)(2,1)}), bf16[32,2,640]{2,1,0:T(2,128)(2,1)S(1)}, u32[]{:S(2)}, u32[]{:S(2)}) %all-to-all-start.1) | async-done | bytes 81952 | tf_op jit(solution)/shard_map/all_to_all | solution.py:133
  48.6 0.2 reshape.181
  48.8 0.3 fusion.45
  49.2 0.1 concatenate.39
  49.3 0.1 concatenate.38
  49.5 0.1 concatenate.40
  49.6 0.1 concatenate.41
  49.7 0.1 concatenate.42
  49.8 0.1 concatenate.43
  49.9 0.1 concatenate.44
  50.0 0.1 concatenate.37
  50.2 0.1 concatenate.45
  50.7 4.5 %fusion.6 = (f32[9,64,512]{2,1,0:T(8,128)}, bf16[9,64,512]{2,1,0:T(8,128)(2,1)S(1)}) fusion(bf16[9,64,576]{2,1,0:T(8,128)(2,1)S(1)} %bitcast_dynamic-update-slice_fusion, bf16[576,512,1]{1,0,2:T(8,128)(2,1)S(1)} %bitcast.85), kind=kOutput, calls=%fused_computation.9 | convolution fusion | flops 361267200 | bytes 3022848 | tf_op jit(solution)/shard_map/psk,kf->psf/dot_general | solution.py:89
  55.2 0.4 pad_convert_fusion
  55.6 1.5 fusion.8
  57.2 92.2 %all-gather.3.cloned.1.call-done = bf16[9216,128]{1,0:T(8,128)(2,1)} async-done(((bf16[288,128]{1,0:T(8,128)(2,1)}), bf16[9216,128]{1,0:T(8,128)(2,1)}) %all-gather.3.cloned.1.call-update) | async-done | bytes 2359312 | tf_op jit(solution)/shard_map/all_gather | solution.py:142
  149.4 0.7 broadcast_in_dim.21.gate_ref
  150.1 4.7 %project.1 = (bf16[9,64,512]{2,1,0:T(8,128)(2,1)}, f32[64,128]{1,0:T(8,128)}) custom-call(bf16[32,288,128]{2,1,0:T(8,128)(2,1)} %bitcast.84, bf16[512,2048]{1,0:T(8,128)(2,1)} %bitcast.86, bf16[9,64,512]{2,1,0:T(8,128)(2,1)} %bitcast.83, f32[64,128]{1,0:T(8,128)} %broadcast_in_dim.21.gate_ref), custom_call_target="tpu_custom_call" | custom-call | tf_op jit(solution)/shard_map/project/pallas_call | solution.py:159
  154.8 0.9 reduce_sum.31
  155.7 0.6 broadcast_in_dim.22
  156.3 12.3 %all-to-all-start.2 = ((f32[32,1,128]{2,1,0:T(1,128)}), f32[32,1,128]{2,1,0:T(1,128)S(1)}, u32[]{:S(2)}, u32[]{:S(2)}) async-start(f32[32,1,128]{2,1,0:T(1,128)} %broadcast_in_dim.22), calls=%async_computation.2 | async-start | bytes 32768 | tf_op jit(solution)/shard_map/all_to_all | solution.py:175
  168.6 3.6 %back.1 = bf16[9,64,64]{2,1,0:T(8,128)(2,1)} custom-call(bf16[9,64,512]{2,1,0:T(8,128)(2,1)} %get-tuple-element.8.refs_0_, f32[9,64,512]{2,1,0:T(8,128)} %get-tuple-element.28.refs_1_, bf16[9,512]{1,0:T(8,128)(2,1)} %bitcast.143, bf16[9,64,512]{2,1,0:T(8,128)(2,1)} %copy-done), custom_call_target="tpu_custom_call" | custom-call | tf_op jit(solution)/shard_map/back/pallas_call | solution.py:179
  172.2 1.0 copy.114
  173.2 0.2 reshape.185
  173.4 16.4 %all-to-all-done.2 = f32[32,1,128]{2,1,0:T(1,128)S(1)} async-done(((f32[32,1,128]{2,1,0:T(1,128)}), f32[32,1,128]{2,1,0:T(1,128)S(1)}, u32[]{:S(2)}, u32[]{:S(2)}) %all-to-all-start.2) | async-done | bytes 16416 | tf_op jit(solution)/shard_map/all_to_all | solution.py:175
  189.9 0.1 copy.100
  190.2 37.0 %all_to_all.21 = bf16[32,2,640]{2,1,0:T(2,128)(2,1)S(1)} all-to-all(bf16[32,2,640]{2,1,0:T(2,128)(2,1)S(1)} %copy.101), channel_id=1, replica_groups=mesh['expert'=32,'chan'=32] {'expert'}, dimensions={0} | all-to-all | bytes 163840 | tf_op jit(solution)/shard_map/all_to_all | solution.py:133
  227.2 0.2 convolution_convert_fusion.2
  227.4 0.7 slice_reduce_fusion
  228.1 0.1 reshape.187
  228.2 0.6 copy.102
  (45 shorter events, 1.0 us)
Async XLA Ops:
  9.7 27.4 %copy-start.2 = (bf16[1,9,512]{2,1,0:T(8,128)(2,1)S(1)}, bf16[1,9,512]{2,1,0:T(8,128)(2,1)}, u32[]{:S(2)}) copy-start(bf16[1,9,512]{2,1,0:T(8,128)(2,1)} %param.12) | copy-start | bytes 27652
  9.8 27.3 %copy-start.1 = (bf16[1,3,3,32,512]{4,3,2,1,0:T(8,128)(2,1)S(1)}, bf16[1,3,3,32,512]{4,3,2,1,0:T(8,128)(2,1)}, u32[]{:S(2)}) copy-start(bf16[1,3,3,32,512]{4,3,2,1,0:T(8,128)(2,1)} %param.11) | copy-start | bytes 884740
  10.8 25.1 %all-to-all-start = ((bf16[32,2,576]{2,1,0:T(2,128)(2,1)}), bf16[32,2,576]{2,1,0:T(2,128)(2,1)S(1)}, u32[]{:S(2)}, u32[]{:S(2)}) async-start(bf16[32,2,576]{2,1,0:T(2,128)(2,1)} %reshape.176), calls=%async_computation | async-start | bytes 163840 | tf_op jit(solution)/shard_map/all_to_all | solution.py:133
  28.4 121.0 %all-gather.3.cloned.1.call-start = ((), (), s32[]{:S(2)}) async-start(), calls=%async_computation.4 | async-start | bytes 2433024 | tf_op jit(solution)/shard_map/all_gather | solution.py:142
  37.2 11.4 %all-to-all-start.1 = ((bf16[32,2,640]{2,1,0:T(2,128)(2,1)}), bf16[32,2,640]{2,1,0:T(2,128)(2,1)S(1)}, u32[]{:S(2)}, u32[]{:S(2)}) async-start(bf16[32,2,640]{2,1,0:T(2,128)(2,1)} %reshape.180), calls=%async_computation.1 | async-start | bytes 163840 | tf_op jit(solution)/shard_map/all_to_all | solution.py:133
  41.1 9.6 %copy-start = (bf16[9,64,512]{2,1,0:T(8,128)(2,1)}, bf16[9,64,512]{2,1,0:T(8,128)(2,1)S(1)}, u32[]{:S(2)}) copy-start(bf16[9,64,512]{2,1,0:T(8,128)(2,1)S(1)} %pad_maximum_fusion.refs_3_) | copy-start | bytes 1769476
  156.3 33.5 %all-to-all-start.2 = ((f32[32,1,128]{2,1,0:T(1,128)}), f32[32,1,128]{2,1,0:T(1,128)S(1)}, u32[]{:S(2)}, u32[]{:S(2)}) async-start(f32[32,1,128]{2,1,0:T(1,128)} %broadcast_in_dim.22), calls=%async_computation.2 | async-start | bytes 32768 | tf_op jit(solution)/shard_map/all_to_all | solution.py:175
Sparse Core Ops, SparseCore 0:
  37.2 112.1 all-gather.2

commit v2 on v1

--- a/solution.py
+++ b/solution.py
@@ -13,18 +13,41 @@
     return row * side + col if 0 <= row < side and 0 <= col < side else None
 
 
-def project_kernel(feat_ref, weight_ref, h_two_ref, gate_ref, d_two_ref, part_ref, left_ref):
-    blocks, rows, lanes = feat_ref.shape
+def project_kernel(
+    turn_ref, own_ref, next_ref, low_ref, high_ref, prev_ref, weight_ref, h_two_ref, gate_ref,
+    d_two_ref, part_ref, left_ref, sums_ref,
+):
+    steps, rows, lanes = own_ref.shape
     half = lanes // 2
     tokens, slots, hidden = d_two_ref.shape
     own = slots // 2
-    for block in range(0, blocks, 2):
-        first = feat_ref[block]
-        second = feat_ref[block + 1]
-        span = slice(block * half, (block + 2) * half)
-        left_ref[:rows, span] = jnp.concatenate([first[:, :half], second[:, :half]], axis=1)
-        left_ref[rows:, span] = jnp.concatenate([first[:, half:], second[:, half:]], axis=1)
+
+    def block(kind, step):
+        if kind == 2:
+            ref, step = (low_ref, step) if step < steps // 2 else (high_ref, step - steps // 2)
+        else:
+            ref = (own_ref, next_ref, None, prev_ref)[kind]
+        return ref[step]
+
+    for turn in range(4):
+
+        @pl.when(turn_ref[0] == turn)
+        def _():
+            for step in range(steps):
+                for pair in range(2):
+                    first = block((2 * pair - turn) % 4, step)
+                    second = block((2 * pair + 1 - turn) % 4, step)
+                    start = (2 * step + pair) * lanes
+                    span = slice(start, start + lanes)
+                    left_ref[:rows, span] = jnp.concatenate(
+                        [first[:, :half], second[:, :half]], axis=1
+                    )
+                    left_ref[rows:, span] = jnp.concatenate(
+                        [first[:, half:], second[:, half:]], axis=1
+                    )
+
     wide = 256
+    sums_ref[...] = jnp.zeros(sums_ref.shape, jnp.float32)
     for group in range(2):
         keep = slice(group * own, (group + 1) * own)
         scale = gate_ref[keep, :][:, :1]
@@ -42,7 +65,15 @@
                 prod = h_two_ref[pos, keep, start : start + wide].astype(jnp.float32) * piece
                 for lane in range(0, wide, 128):
                     total = total + prod[:, lane : lane + 128]
-        part_ref[keep, :] = total
+        sums_ref[keep, :] = total
+    row = lax.dot_general(
+        jnp.ones((8, 128), jnp.float32),
+        sums_ref[...],
+        (((1,), (1,)), ((), ())),
+        preferred_element_type=jnp.float32,
+        precision=lax.Precision.HIGHEST,
+    )[:1]
+    part_ref[...] = jnp.broadcast_to(row[None], part_ref.shape)
 
 
 def back_kernel(d_two_ref, slope_ref, taps_ref, kernel_ref, d_in_ref, d_one_ref, *, side):
@@ -133,18 +164,31 @@
         return lax.all_to_all(array, "expert", split_axis=0, concat_axis=0, tiled=True)
 
     tail = 64
-    grads = exchange(place(grad_out.reshape(owned, width)))
-    packed = grads.reshape(sections, CAP, tokens, feat).transpose(2, 0, 1, 3)
+    both = 2 * width
+    extra = jnp.pad(gate[:, None], ((0, 0), (0, tail - 1)))
+    flat = jnp.concatenate(
+        [grad_out.reshape(owned, width), tiles_in.reshape(owned, width), extra], axis=1
+    )
+    arrived = exchange(place(flat))
+    packed = arrived[:, :, :width].reshape(sections, CAP, tokens, feat).transpose(2, 0, 1, 3)
     packed = packed.reshape(tokens * sections, CAP * feat)
-    extra = jnp.pad(gate[:, None], ((0, 0), (0, tail - 1)))
-    outward = place(jnp.concatenate([tiles_in.reshape(owned, width), extra], axis=1))
-    packed, outward = lax.optimization_barrier((packed, outward))
-    gathered = lax.all_gather(packed, "chan", axis=0, tiled=False)
-    arrived = exchange(outward)
-
-    inputs = arrived[:, :, :width].reshape(sections, CAP, tokens, feat).transpose(2, 1, 0, 3)
+    chans = lax.axis_size("chan")
+    steps = chans // 4
+    families = [[4 * step + kind for step in range(steps)] for kind in range(4)]
+    own = lax.all_gather(packed, "chan", axis=0, axis_index_groups=families)
+
+    def shift(array, by):
+        return lax.ppermute(array, "chan", [(c, (c + by) % chans) for c in range(chans)])
+
+    low = shift(own[: steps // 2], 2)
+    high = shift(own[steps // 2 :], -2)
+    prev = shift(own, 1)
+    following = shift(own, -1)
+    turn = (lax.axis_index("chan") % 4).astype(jnp.int32).reshape(1)
+
+    inputs = arrived[:, :, width:both].reshape(sections, CAP, tokens, feat).transpose(2, 1, 0, 3)
     inputs = inputs.reshape(tokens, slots, feat)
-    gates = arrived[:, :, width].T.reshape(slots, 1).astype(jnp.float32)
+    gates = arrived[:, :, both].T.reshape(slots, 1).astype(jnp.float32)
     gates = jnp.broadcast_to(gates, (slots, 128))
     taps = w_depth[0]
     small = w_conv[0].reshape(9, group, hidden)
@@ -160,22 +204,18 @@
         project_kernel,
         out_shape=(
             jax.ShapeDtypeStruct((tokens, slots, hidden), jnp.bfloat16),
-            jax.ShapeDtypeStruct((slots, 128), jnp.float32),
+            jax.ShapeDtypeStruct((chans, 1, 128), jnp.float32),
         ),
-        in_specs=vmem(4),
+        in_specs=[pl.BlockSpec(memory_space=pltpu.SMEM)] + vmem(8),
         out_specs=tuple(vmem(2)),
         scratch_shapes=[
             pltpu.VMEM((tokens * slots, w_out.shape[2]), jnp.bfloat16),
+            pltpu.VMEM((128, 128), jnp.float32),
         ],
         name="project",
-    )(gathered, w_out[0], h_two, gates)
-    part = jnp.sum(part, axis=1)
-    part = jnp.pad(part, (0, 128 - slots))
-    chans = lax.axis_size("chan")
-    parts = lax.all_to_all(
-        jnp.broadcast_to(part[None], (chans, 128)), "chan", split_axis=0, concat_axis=0, tiled=True
-    )
-    gate_grad = jnp.sum(parts, axis=0)[:slots].astype(jnp.bfloat16)
+    )(turn, own, following, low, high, prev, w_out[0], h_two, gates)
+    parts = lax.all_to_all(part, "chan", split_axis=0, concat_axis=0, tiled=True)
+    gate_grad = jnp.sum(parts[:, 0], axis=0)[:slots].astype(jnp.bfloat16)
     d_input = pl.pallas_call(
         lambda *refs: back_kernel(*refs, side=side),
         out_shape=jax.ShapeDtypeStruct((tokens, slots, feat), jnp.bfloat16),

time: 236 us -> 169 us (0.72)
  waiting for transfers between devices: 121 us -> 23.7 us
  blocking collectives: 37 us -> 62.8 us
  between operations: 14.4 us -> 1.07 us
  starting transfers between devices: 33.9 us -> 44.4 us
  local copies, waits for them, and re-layouts: 11.5 us -> 16.9 us
    all_gather x1 -> x0, waiting for transfers between devices: 92.2 us -> none  [on_device(): gathered = lax.all_gather(packed, 'chan', axis=0, tiled=False)]
    all_gather x0 -> x1, blocking collectives: none -> 43.5 us  [on_device(): own = lax.all_gather(packed, 'chan', axis=0, axis_index_groups=families)]
    all_to_all x1, blocking collectives: 37 us -> 19.3 us  [exchange(): lax.all_to_all(array, 'expert', split_axis=0, concat_axis=0, tiled=True)]
    ppermute x0 -> x4, starting transfers between devices: none -> 14 us  [shift(): lax.ppermute(array, 'chan', [(c, (c + by) % chans) for c in range(chans)])]
    unnamed x27 -> x55, local copies, waits for them, and re-layouts: 2.79 us -> 8.23 us
    all_to_all x2 -> x1, waiting for transfers between devices: 12.2 us -> 7.29 us  [exchange(): lax.all_to_all(array, 'expert', split_axis=0, concat_axis=0, tiled=True)]
    all_to_all x2 -> x1, starting transfers between devices: 21.5 us -> 17.6 us  [exchange(): lax.all_to_all(array, 'expert', split_axis=0, concat_axis=0, tiled=True)]
  transfers between devices with their start and end apart: 4 -> 6, of which waited for: 4 -> 2; matrix products, arithmetic and copies ran while one was open for 5% -> 9% of each run, Pallas kernels for 2% -> 2%
where the time goes in v2:
time: 169 us; the launch traced here: 168 us
  blocking collectives  62.8 us (37%)
  starting transfers between devices  44.4 us (26%)
  waiting for transfers between devices  23.7 us (14%)
  local copies, waits for them, and re-layouts  16.9 us (10%)
  Pallas kernels  9.11 us (5%)
  matrix products  5.9 us (3%)
  other arithmetic  4.37 us (3%)
    all_gather x1, blocking collectives, on_device(): own = lax.all_gather(packed, 'chan', axis=0, axis_index_groups=families)  43.5 us
    all_to_all x1, blocking collectives, exchange(): lax.all_to_all(array, 'expert', split_axis=0, concat_axis=0, tiled=True)  19.3 us
    all_to_all x1, starting transfers between devices, exchange(): lax.all_to_all(array, 'expert', split_axis=0, concat_axis=0, tiled=True)  17.6 us
    all_to_all x1, waiting for transfers between devices, on_device(): lax.all_to_all(part, 'chan', split_axis=0, concat_axis=0, tiled=True)  16.4 us
    ppermute x4, starting transfers between devices, shift(): lax.ppermute(array, 'chan', [(c, (c + by) % chans) for c in range(chans)])  14 us
    all_to_all x1, starting transfers between devices, on_device(): lax.all_to_all(part, 'chan', split_axis=0, concat_axis=0, tiled=True)  12.8 us
    unnamed x55, local copies, waits for them, and re-layouts  8.23 us
    all_to_all x1, waiting for transfers between devices, exchange(): lax.all_to_all(array, 'expert', split_axis=0, concat_axis=0, tiled=True)  7.29 us
  transfers between devices with their start and end apart: 6, of which 2 were waited for; matrix products, arithmetic and copies ran while one was open for 9% of the time, Pallas kernels for 2%

profile of v2, /device:TPU:1, one launch (start us, length us, event | category | flops | bytes accessed | tf_op | source)
XLA Modules:
  0.0 168.2 jit_solution(17112507451863929624)
XLA Ops:
  0.6 0.9 convert_reduce_fusion
  1.5 0.7 fusion.33
  2.2 0.9 copy.76
  3.2 0.1 reshape.167
  3.3 0.9 copy.77
  4.2 0.1 reshape.168
  4.4 0.8 copy.78
  5.2 0.3 convolution_convert_fusion
  5.5 0.7 reshape.169
  6.3 17.6 %all-to-all-start = ((bf16[32,2,1216]{2,1,0:T(2,128)(2,1)}), bf16[32,2,1216]{2,1,0:T(2,128)(2,1)S(1)}, u32[]{:S(2)}, u32[]{:S(2)}) async-start(bf16[32,2,1216]{2,1,0:T(2,128)(2,1)} %reshape.169), calls=%async_computation | async-start | bytes 327680 | tf_op jit(solution)/shard_map/all_to_all | solution.py:164
  24.0 0.6 slice_convert_fusion.8
  24.7 7.3 %all-to-all-done = bf16[32,2,1216]{2,1,0:T(2,128)(2,1)S(1)} async-done(((bf16[32,2,1216]{2,1,0:T(2,128)(2,1)}), bf16[32,2,1216]{2,1,0:T(2,128)(2,1)S(1)}, u32[]{:S(2)}, u32[]{:S(2)}) %all-to-all-start) | async-done | bytes 155680 | tf_op jit(solution)/shard_map/all_to_all | solution.py:164
  32.0 0.2 fusion.36
  32.2 0.2 reshape.171
  32.4 0.3 fusion.35
  33.9 0.2 reshape.170
  34.0 0.2 copy.80
  34.3 43.5 %all_gather.3.own_ref = bf16[8,288,128]{2,1,0:T(8,128)(2,1)S(1)} all-gather(bf16[1,288,128]{2,1,0:T(8,128)(2,1)S(1)} %all_gather_reshape.3), channel_id=1, replica_groups={{0,4,8,12,16,20,24,28},{1,5,9,13,17,21,25,29},{2,6,10,14,18,22,26,30},{..., dimensions={0}, use_global_device_ids=true | all-gather | bytes 663552 | tf_op jit(solution)/shard_map/all_gather | solution.py:178
  77.8 0.8 fusion.34
  78.7 4.7 %collective-permute-start = (bf16[8,288,128]{2,1,0:T(8,128)(2,1)S(1)}, bf16[8,288,128]{2,1,0:T(8,128)(2,1)S(1)}, u32[]{:S(2)}, u32[]{:S(2)}) collective-permute-start(bf16[8,288,128]{2,1,0:T(8,128)(2,1)S(1)} %all_gather.3.own_ref), channel_id=1, source_target_pairs={{0,31},{1,0},{2,1},{3,2},{4,3},{5,4},{6,5},{7,6},{8,7},{9,8},{10,9... | collective-permute-start | bytes 1769480 | tf_op jit(solution)/shard_map/ppermute | solution.py:181
  83.4 1.9 %collective-permute-start.3 = (bf16[8,288,128]{2,1,0:T(8,128)(2,1)S(1)}, bf16[8,288,128]{2,1,0:T(8,128)(2,1)S(1)}, u32[]{:S(2)}, u32[]{:S(2)}) collective-permute-start(bf16[8,288,128]{2,1,0:T(8,128)(2,1)S(1)} %all_gather.3.own_ref), channel_id=1, source_target_pairs={{0,1},{1,2},{2,3},{3,4},{4,5},{5,6},{6,7},{7,8},{8,9},{9,10},{10,1... | collective-permute-start | bytes 1769480 | tf_op jit(solution)/shard_map/ppermute | solution.py:181
  85.3 0.6 bitcast_dynamic-update-slice_fusion.8
  85.9 3.0 %collective-permute-start.1 = (bf16[4,288,128]{2,1,0:T(8,128)(2,1)}, bf16[4,288,128]{2,1,0:T(8,128)(2,1)}, u32[]{:S(2)}, u32[]{:S(2)}) collective-permute-start(bf16[4,288,128]{2,1,0:T(8,128)(2,1)} %get-tuple-element.25), channel_id=1, source_target_pairs={{0,2},{1,3},{2,4},{3,5},{4,6},{5,7},{6,8},{7,9},{8,10},{9,11},{10,... | collective-permute-start | bytes 884744 | tf_op jit(solution)/shard_map/ppermute | solution.py:181
  88.9 4.4 %collective-permute-start.2 = (bf16[4,288,128]{2,1,0:T(8,128)(2,1)S(1)}, bf16[4,288,128]{2,1,0:T(8,128)(2,1)}, u32[]{:S(2)}, u32[]{:S(2)}) collective-permute-start(bf16[4,288,128]{2,1,0:T(8,128)(2,1)S(1)} %get-tuple-element.24), channel_id=1, source_target_pairs={{0,30},{1,31},{2,0},{3,1},{4,2},{5,3},{6,4},{7,5},{8,6},{9,7},{10,... | collective-permute-start | bytes 884744 | tf_op jit(solution)/shard_map/ppermute | solution.py:181
  93.4 0.6 bitcast_dynamic-update-slice_fusion.7
  94.1 0.6 bitcast_dynamic-update-slice_fusion.6
  94.7 0.6 bitcast_dynamic-update-slice_fusion.5
  95.3 0.6 bitcast_dynamic-update-slice_fusion.4
  96.0 0.6 bitcast_dynamic-update-slice_fusion.3
  96.6 0.6 bitcast_dynamic-update-slice_fusion.2
  97.3 0.6 bitcast_dynamic-update-slice_fusion.1
  97.9 0.6 bitcast_dynamic-update-slice_fusion
  98.5 5.4 %fusion.6 = (f32[9,64,512]{2,1,0:T(8,128)}, bf16[9,64,512]{2,1,0:T(8,128)(2,1)S(1)}) fusion(bf16[9,64,576]{2,1,0:T(8,128)(2,1)} %bitcast_dynamic-update-slice_fusion, bf16[576,512,1]{1,0,2:T(8,128)(2,1)S(1)} %bitcast.82), kind=kOutput, calls=%fused_computation.10 | convolution fusion | flops 361267200 | bytes 3022848 | tf_op jit(solution)/shard_map/psk,kf->psf/dot_general | solution.py:120
  104.1 0.4 pad_convert_fusion
  104.5 0.2 copy-done.6
  104.8 1.5 fusion.8
  106.3 0.8 broadcast_in_dim.19.gate_ref
  107.1 0.2 copy-done.3
  107.3 5.5 %project.1 = (bf16[9,64,512]{2,1,0:T(8,128)(2,1)}, f32[32,1,128]{2,1,0:T(1,128)}) custom-call(s32[1]{0:T(128)} %bitcast.3.turn_ref, bf16[8,288,128]{2,1,0:T(8,128)(2,1)} %copy-done, bf16[8,288,128]{2,1,0:T(8,128)(2,1)} %copy-done.2, bf16[4,288,128]{2,1,0:T(8,128)(2,1)} %collective-permute-done.1.low_ref, ...), custom_call_target="tpu_custom_call" | custom-call | tf_op jit(solution)/shard_map/project/pallas_call | solution.py:203
  112.8 12.8 %all-to-all-start.1 = ((f32[32,1,128]{2,1,0:T(1,128)}), f32[32,1,128]{2,1,0:T(1,128)S(1)}, u32[]{:S(2)}, u32[]{:S(2)}) async-start(f32[32,1,128]{2,1,0:T(1,128)} %get-tuple-element.5), calls=%async_computation.1 | async-start | bytes 32768 | tf_op jit(solution)/shard_map/all_to_all | solution.py:217
  125.6 3.6 %back.1 = bf16[9,64,64]{2,1,0:T(8,128)(2,1)} custom-call(bf16[9,64,512]{2,1,0:T(8,128)(2,1)} %get-tuple-element.4.refs_0_, f32[9,64,512]{2,1,0:T(8,128)} %get-tuple-element.22.refs_1_, bf16[9,512]{1,0:T(8,128)(2,1)} %bitcast.139, bf16[9,64,512]{2,1,0:T(8,128)(2,1)} %copy-done.1), custom_call_target="tpu_custom_call" | custom-call | tf_op jit(solution)/shard_map/back/pallas_call | solution.py:219
  129.2 1.0 copy.98
  130.2 0.2 reshape.175
  130.4 16.4 %all-to-all-done.1 = f32[32,1,128]{2,1,0:T(1,128)S(1)} async-done(((f32[32,1,128]{2,1,0:T(1,128)}), f32[32,1,128]{2,1,0:T(1,128)S(1)}, u32[]{:S(2)}, u32[]{:S(2)}) %all-to-all-start.1) | async-done | bytes 16416 | tf_op jit(solution)/shard_map/all_to_all | solution.py:217
  147.2 19.3 %all_to_all.15 = bf16[32,2,640]{2,1,0:T(2,128)(2,1)S(1)} all-to-all(bf16[32,2,640]{2,1,0:T(2,128)(2,1)S(1)} %copy.85), channel_id=1, replica_groups=mesh['expert'=32,'chan'=32] {'expert'}, dimensions={0} | all-to-all | bytes 163840 | tf_op jit(solution)/shard_map/all_to_all | solution.py:164
  166.6 0.2 convolution_convert_fusion.1
  166.8 0.7 slice_reduce_fusion
  167.6 0.6 copy.86
  (76 shorter events, 2.3 us)
Async XLA Ops:
  0.6 23.3 %copy-start.4 = (bf16[1,3,3,32,512]{4,3,2,1,0:T(8,128)(2,1)S(1)}, bf16[1,3,3,32,512]{4,3,2,1,0:T(8,128)(2,1)}, u32[]{:S(2)}) copy-start(bf16[1,3,3,32,512]{4,3,2,1,0:T(8,128)(2,1)} %param.11) | copy-start | bytes 884740
  2.2 21.8 %copy-start.15 = (s32[32]{0:T(128)}, s32[32]{0:T(128)S(1)}, u32[]{:S(2)}) copy-start(s32[32]{0:T(128)S(1)} %fusion.33) | copy-start | bytes 388
  3.3 20.7 %copy-start.5 = (bf16[1,9,512]{2,1,0:T(8,128)(2,1)S(1)}, bf16[1,9,512]{2,1,0:T(8,128)(2,1)}, u32[]{:S(2)}) copy-start(bf16[1,9,512]{2,1,0:T(8,128)(2,1)} %param.12) | copy-start | bytes 27652
  6.3 25.7 %all-to-all-start = ((bf16[32,2,1216]{2,1,0:T(2,128)(2,1)}), bf16[32,2,1216]{2,1,0:T(2,128)(2,1)S(1)}, u32[]{:S(2)}, u32[]{:S(2)}) async-start(bf16[32,2,1216]{2,1,0:T(2,128)(2,1)} %reshape.169), calls=%async_computation | async-start | bytes 327680 | tf_op jit(solution)/shard_map/all_to_all | solution.py:164
  24.7 73.8 %copy-start.1 = (bf16[9,64,512]{2,1,0:T(8,128)(2,1)}, bf16[9,64,512]{2,1,0:T(8,128)(2,1)S(1)}, u32[]{:S(2)}) copy-start(bf16[9,64,512]{2,1,0:T(8,128)(2,1)S(1)} %pad_maximum_fusion.refs_3_) | copy-start | bytes 1769476
  77.8 19.4 %copy-start = (bf16[8,288,128]{2,1,0:T(8,128)(2,1)}, bf16[8,288,128]{2,1,0:T(8,128)(2,1)S(1)}, u32[]{:S(2)}) copy-start(bf16[8,288,128]{2,1,0:T(8,128)(2,1)S(1)} %all_gather.3.own_ref) | copy-start | bytes 1769476
  78.7 27.6 %collective-permute-start = (bf16[8,288,128]{2,1,0:T(8,128)(2,1)S(1)}, bf16[8,288,128]{2,1,0:T(8,128)(2,1)S(1)}, u32[]{:S(2)}, u32[]{:S(2)}) collective-permute-start(bf16[8,288,128]{2,1,0:T(8,128)(2,1)S(1)} %all_gather.3.own_ref), channel_id=1, source_target_pairs={{0,31},{1,0},{2,1},{3,2},{4,3},{5,4},{6,5},{7,6},{8,7},{9,8},{10,9... | collective-permute-start | bytes 1769480 | tf_op jit(solution)/shard_map/ppermute | solution.py:181
  83.4 22.9 %collective-permute-start.3 = (bf16[8,288,128]{2,1,0:T(8,128)(2,1)S(1)}, bf16[8,288,128]{2,1,0:T(8,128)(2,1)S(1)}, u32[]{:S(2)}, u32[]{:S(2)}) collective-permute-start(bf16[8,288,128]{2,1,0:T(8,128)(2,1)S(1)} %all_gather.3.own_ref), channel_id=1, source_target_pairs={{0,1},{1,2},{2,3},{3,4},{4,5},{5,6},{6,7},{7,8},{8,9},{9,10},{10,1... | collective-permute-start | bytes 1769480 | tf_op jit(solution)/shard_map/ppermute | solution.py:181
  85.9 20.3 %collective-permute-start.1 = (bf16[4,288,128]{2,1,0:T(8,128)(2,1)}, bf16[4,288,128]{2,1,0:T(8,128)(2,1)}, u32[]{:S(2)}, u32[]{:S(2)}) collective-permute-start(bf16[4,288,128]{2,1,0:T(8,128)(2,1)} %get-tuple-element.25), channel_id=1, source_target_pairs={{0,2},{1,3},{2,4},{3,5},{4,6},{5,7},{6,8},{7,9},{8,10},{9,11},{10,... | collective-permute-start | bytes 884744 | tf_op jit(solution)/shard_map/ppermute | solution.py:181
  88.9 17.4 %collective-permute-start.2 = (bf16[4,288,128]{2,1,0:T(8,128)(2,1)S(1)}, bf16[4,288,128]{2,1,0:T(8,128)(2,1)}, u32[]{:S(2)}, u32[]{:S(2)}) collective-permute-start(bf16[4,288,128]{2,1,0:T(8,128)(2,1)S(1)} %get-tuple-element.24), channel_id=1, source_target_pairs={{0,30},{1,31},{2,0},{3,1},{4,2},{5,3},{6,4},{7,5},{8,6},{9,7},{10,... | collective-permute-start | bytes 884744 | tf_op jit(solution)/shard_map/ppermute | solution.py:181
  104.0 0.7 copy-start.6
  104.0 0.7 copy-start.7
  104.0 0.7 copy-start.8
  104.0 0.7 copy-start.9
  104.0 0.7 copy-start.10
  104.0 0.7 copy-start.11
  104.0 0.7 copy-start.12
  104.1 0.7 copy-start.13
  104.1 0.7 copy-start.14
  106.3 0.8 copy-start.2
  106.3 1.0 copy-start.3
  112.8 34.0 %all-to-all-start.1 = ((f32[32,1,128]{2,1,0:T(1,128)}), f32[32,1,128]{2,1,0:T(1,128)S(1)}, u32[]{:S(2)}, u32[]{:S(2)}) async-start(f32[32,1,128]{2,1,0:T(1,128)} %get-tuple-element.5), calls=%async_computation.1 | async-start | bytes 32768 | tf_op jit(solution)/shard_map/all_to_all | solution.py:217
  129.2 37.3 %copy-start.16 = (s32[32]{0:T(128)S(1)}, s32[32]{0:T(128)}, u32[]{:S(2)}) copy-start(s32[32]{0:T(128)} %copy-done.15) | copy-start | bytes 388

commit v3 on v2

--- a/solution.py
+++ b/solution.py
@@ -11,6 +11,83 @@
 def near(pos, off, side):
     row, col = pos // side + off // 3 - 1, pos % side + off % 3 - 1
     return row * side + col if 0 <= row < side and 0 <= col < side else None
+
+
+def prep_kernel(ids_ref, gate_ref, grads_ref, tiles_ref, out_ref):
+    tokens, owned, feat = grads_ref.shape
+    sections = out_ref.shape[0]
+    ids = ids_ref[...]
+    rows = lax.broadcasted_iota(jnp.int32, (owned, owned), 0)
+    cols = lax.broadcasted_iota(jnp.int32, (owned, owned), 1)
+    wide = jnp.broadcast_to(ids, (owned, owned))
+    column = jnp.sum(jnp.where(rows == cols, wide, 0), axis=1, keepdims=True)
+    earlier = jnp.where((rows < cols) & (column == wide), 1, 0)
+    rank = jnp.sum(earlier, axis=0, keepdims=True)
+    named = jnp.broadcast_to(ids, (sections, owned)) == lax.broadcasted_iota(
+        jnp.int32, (sections, owned), 0
+    )
+    turn = jnp.broadcast_to(rank, (sections, owned))
+    picks = [jnp.where(named & (turn == r), 1.0, 0.0).astype(jnp.bfloat16) for r in range(CAP)]
+    gates = jnp.broadcast_to(gate_ref[...].astype(jnp.float32), (owned, owned))
+    gates = jnp.sum(jnp.where(rows == cols, gates, 0.0), axis=1, keepdims=True)
+    gates = jnp.broadcast_to(gates, (owned, feat)).astype(jnp.bfloat16)
+    fields = [grads_ref[pos] for pos in range(tokens)]
+    fields += [tiles_ref[pos] for pos in range(tokens)] + [gates]
+    lines = []
+    for field in fields:
+        halves = [jnp.dot(pick, field, preferred_element_type=jnp.float32) for pick in picks]
+        lines.append(jnp.concatenate(halves, axis=1))
+    while len(lines) < out_ref.shape[1]:
+        lines.append(jnp.zeros_like(lines[0]))
+    out_ref[...] = jnp.swapaxes(jnp.stack(lines), 0, 1).astype(jnp.bfloat16)
+
+
+def sort_kernel(in_ref, packed_ref, inputs_ref, gates_ref):
+    tokens, slots, feat = inputs_ref.shape
+    own = slots // 2
+    lines = jnp.swapaxes(in_ref[...].astype(jnp.float32), 0, 1)
+    for pos in range(tokens):
+        packed_ref[pos * own : (pos + 1) * own, :] = lines[pos].astype(jnp.bfloat16)
+        field = lines[tokens + pos]
+        inputs_ref[pos] = jnp.concatenate([field[:, :feat], field[:, feat:]], axis=0).astype(
+            jnp.bfloat16
+        )
+    field = lines[2 * tokens]
+    for group in range(2):
+        part = field[:, group * feat : (group + 1) * feat]
+        gates_ref[group * own : (group + 1) * own, :] = jnp.concatenate([part, part], axis=1)
+
+
+def forward_kernel(
+    inputs_ref, kernel_ref, taps_ref, h_two_ref, slope_ref, act_ref, *, side
+):
+    tokens, slots, hidden = h_two_ref.shape
+    wide = 256
+    for start in range(0, hidden, wide):
+        span = slice(start, start + wide)
+        for pos in range(tokens):
+            value = jnp.zeros((slots, wide), jnp.float32)
+            for off in range(9):
+                other = near(pos, off, side)
+                if other is not None:
+                    value = value + jnp.dot(
+                        inputs_ref[other],
+                        kernel_ref[off, :, span],
+                        preferred_element_type=jnp.float32,
+                    )
+            cdf = 0.5 * (1.0 + lax.erf(value * 0.7071067811865476))
+            act_ref[pos, :, span] = (value * cdf).astype(jnp.bfloat16).astype(jnp.float32)
+            slope_ref[pos, :, span] = (
+                cdf + value * jnp.exp(-0.5 * value * value) * 0.3989422804014327
+            )
+        taps = [taps_ref[off : off + 1, span].astype(jnp.float32) for off in range(9)]
+        for pos in range(tokens):
+            total = jnp.zeros((slots, wide), jnp.float32)
+            for off in range(9):
+                other = near(pos, off, side)
+                if other is not None:
+                    total = total + act_ref[other, :, span] * taps[off]
+            h_two_ref[pos, :, span] = total.astype(jnp.bfloat16)
 
 
 def project_kernel(
@@ -108,36 +185,6 @@
     return [pl.BlockSpec(memory_space=pltpu.VMEM) for _ in range(count)]
 
 
-def forward(inputs, kernel, taps, side):
-    tokens = side * side
-    blank = jnp.zeros_like(inputs[0])
-    columns = []
-    for pos in range(tokens):
-        picked = [near(pos, off, side) for off in range(9)]
-        columns.append(
-            jnp.concatenate([blank if n is None else inputs[n] for n in picked], axis=1)
-        )
-    h_one = jnp.einsum(
-        "psk,kf->psf",
-        jnp.stack(columns),
-        kernel.reshape(-1, kernel.shape[2]),
-        preferred_element_type=jnp.float32,
-    )
-    active = jax.nn.gelu(h_one, approximate=False).astype(jnp.bfloat16)
-    grid = active.reshape(side, side, *active.shape[1:])
-    padded = jnp.pad(grid, ((1, 1), (1, 1), (0, 0), (0, 0))).astype(jnp.float32)
-    total = jnp.zeros(grid.shape, jnp.float32)
-    for row in range(3):
-        for col in range(3):
-            total = total + padded[row : row + side, col : col + side] * taps[3 * row + col].astype(
-                jnp.float32
-            )
-    h_two = total.reshape(active.shape).astype(jnp.bfloat16)
-    cdf = 0.5 * (1.0 + lax.erf(h_one * 0.7071067811865476))
-    slope = cdf + h_one * jnp.exp(-0.5 * h_one * h_one) * 0.3989422804014327
-    return h_two, slope
-
-
 def on_device(tiles_in, grad_out, gate, expert_id, w_conv, w_depth, w_out):
     owned, side, _, feat = tiles_in.shape
     tokens = side * side
@@ -154,24 +201,35 @@
     slot = chosen * CAP + rank
     placing = (slot[:, None] == jnp.arange(slots, dtype=jnp.int32)[None, :]).astype(jnp.bfloat16)
 
-    def place(array):
-        out = lax.dot_general(
-            placing, array, (((0,), (0,)), ((), ())), preferred_element_type=jnp.float32
-        )
-        return out.astype(jnp.bfloat16).reshape(sections, CAP, -1)
-
     def exchange(array):
         return lax.all_to_all(array, "expert", split_axis=0, concat_axis=0, tiled=True)
 
     tail = 64
-    both = 2 * width
-    extra = jnp.pad(gate[:, None], ((0, 0), (0, tail - 1)))
-    flat = jnp.concatenate(
-        [grad_out.reshape(owned, width), tiles_in.reshape(owned, width), extra], axis=1
-    )
-    arrived = exchange(place(flat))
-    packed = arrived[:, :, :width].reshape(sections, CAP, tokens, feat).transpose(2, 0, 1, 3)
-    packed = packed.reshape(tokens * sections, CAP * feat)
+    lines = -(-(2 * tokens + 1) // 8) * 8
+    outward = pl.pallas_call(
+        prep_kernel,
+        out_shape=jax.ShapeDtypeStruct((sections, lines, CAP * feat), jnp.bfloat16),
+        in_specs=vmem(4),
+        out_specs=vmem(1)[0],
+        name="prep",
+    )(
+        expert_id.reshape(1, owned),
+        gate.reshape(1, owned),
+        grad_out.transpose(1, 2, 0, 3).reshape(tokens, owned, feat),
+        tiles_in.transpose(1, 2, 0, 3).reshape(tokens, owned, feat),
+    )
+    arrived = exchange(outward)
+    packed, inputs, gates = pl.pallas_call(
+        sort_kernel,
+        out_shape=(
+            jax.ShapeDtypeStruct((tokens * sections, CAP * feat), jnp.bfloat16),
+            jax.ShapeDtypeStruct((tokens, slots, feat), jnp.bfloat16),
+            jax.ShapeDtypeStruct((slots, 128), jnp.float32),
+        ),
+        in_specs=vmem(1),
+        out_specs=tuple(vmem(3)),
+        name="sort",
+    )(arrived)
     chans = lax.axis_size("chan")
     steps = chans // 4
     families = [[4 * step + kind for step in range(steps)] for kind in range(4)]
@@ -186,10 +244,6 @@
     following = shift(own, -1)
     turn = (lax.axis_index("chan") % 4).astype(jnp.int32).reshape(1)
 
-    inputs = arrived[:, :, width:both].reshape(sections, CAP, tokens, feat).transpose(2, 1, 0, 3)
-    inputs = inputs.reshape(tokens, slots, feat)
-    gates = arrived[:, :, both].T.reshape(slots, 1).astype(jnp.float32)
-    gates = jnp.broadcast_to(gates, (slots, 128))
     taps = w_depth[0]
     small = w_conv[0].reshape(9, group, hidden)
     count = feat // group
@@ -198,7 +252,17 @@
     kernel = jnp.concatenate(
         [jnp.where(which == g, small, jnp.zeros_like(small)) for g in range(count)], axis=1
     )
-    h_two, slope = forward(inputs, kernel, taps, side)
+    h_two, slope = pl.pallas_call(
+        lambda *refs: forward_kernel(*refs, side=side),
+        out_shape=(
+            jax.ShapeDtypeStruct((tokens, slots, hidden), jnp.bfloat16),
+            jax.ShapeDtypeStruct((tokens, slots, hidden), jnp.float32),
+        ),
+        in_specs=vmem(3),
+        out_specs=tuple(vmem(2)),
+        scratch_shapes=[pltpu.VMEM((tokens, slots, hidden), jnp.float32)],
+        name="forward",
+    )(inputs, kernel, taps)
 
     d_two, part = pl.pallas_call(
         project_kernel,

time: 169 us -> 166 us (0.982)
  blocking collectives: 62.8 us -> 43.7 us
  waiting for transfers between devices: 23.7 us -> 38.6 us
  starting transfers between devices: 44.4 us -> 59 us
  local copies, waits for them, and re-layouts: 16.9 us -> 5.44 us
  Pallas kernels: 9.11 us -> 16.4 us
  matrix products: 5.9 us -> 0.19 us
  other arithmetic: 4.37 us -> 1.27 us
    all_to_all x1 -> x0, blocking collectives: 19.3 us -> none  [exchange(): lax.all_to_all(array, 'expert', split_axis=0, concat_axis=0, tiled=True)]
    all_to_all x1 -> x2, starting transfers between devices: 17.6 us -> 32 us  [exchange(): lax.all_to_all(array, 'expert', split_axis=0, concat_axis=0, tiled=True)]
    all_to_all x1 -> x2, waiting for transfers between devices: 7.29 us -> 15.8 us  [exchange(): lax.all_to_all(array, 'expert', split_axis=0, concat_axis=0, tiled=True)]
    pallas_call x0 -> x3, Pallas kernels: none -> 7.29 us  [the longest x1 3.51 us: on_device(): pl.pallas_call(lambda *refs: forward_kernel(*refs, side=side), out_shape=...]
    ppermute x4, waiting for transfers between devices: 0.01 us -> 6.65 us  [shift(): lax.ppermute(array, 'chan', [(c, (c + by) % chans) for c in range(chans)])]
    unnamed x55 -> x17, local copies, waits for them, and re-layouts: 8.23 us -> 2.44 us
    dot_general x2 -> x0, matrix products: 5.71 us -> none  [the longest x1 5.4 us: forward(): jnp.einsum('psk,kf->psf', jnp.stack(columns), kernel.reshape(-1, kernel.s...]
    convert_element_type x4 -> x0, other arithmetic: 2.55 us -> none  [the longest x1 1.5 us: forward(): h_two = total.reshape(active.shape).astype(jnp.bfloat16)]
  transfers between devices with their start and end apart: 6 -> 7, of which waited for: 2 -> 5; matrix products, arithmetic and copies ran while one was open for 9% -> 1% of each run, Pallas kernels for 2% -> 4%
where the time goes in v3:
time: 166 us; the launch traced here: 165 us
  starting transfers between devices  59 us (36%)
  blocking collectives  43.7 us (26%)
  waiting for transfers between devices  38.6 us (23%)
  Pallas kernels  16.4 us (10%)
  local copies, waits for them, and re-layouts  5.44 us (3%)
    all_gather x1, blocking collectives, on_device(): own = lax.all_gather(packed, 'chan', axis=0, axis_index_groups=families)  43.7 us
    all_to_all x2, starting transfers between devices, exchange(): lax.all_to_all(array, 'expert', split_axis=0, concat_axis=0, tiled=True)  32 us
    all_to_all x1, waiting for transfers between devices, on_device(): lax.all_to_all(part, 'chan', split_axis=0, concat_axis=0, tiled=True)  16.2 us
    all_to_all x2, waiting for transfers between devices, exchange(): lax.all_to_all(array, 'expert', split_axis=0, concat_axis=0, tiled=True)  15.8 us
    ppermute x4, starting transfers between devices, shift(): lax.ppermute(array, 'chan', [(c, (c + by) % chans) for c in range(chans)])  13.7 us
    all_to_all x1, starting transfers between devices, on_device(): lax.all_to_all(part, 'chan', split_axis=0, concat_axis=0, tiled=True)  13.3 us
    ppermute x4, waiting for transfers between devices, shift(): lax.ppermute(array, 'chan', [(c, (c + by) % chans) for c in range(chans)])  6.65 us
    pallas_call x1, Pallas kernels, on_device(): pl.pallas_call(project_kernel, out_shape=(jax.ShapeDtypeStruct((tokens, s...  5.56 us
  transfers between devices with their start and end apart: 7, of which 5 were waited for; matrix products, arithmetic and copies ran while one was open for 1% of the time, Pallas kernels for 4%

profile of v3, /device:TPU:1, one launch (start us, length us, event | category | flops | bytes accessed | tf_op | source)
XLA Modules:
  0.0 165.4 jit_solution(10828621574746515899)
XLA Ops:
  0.6 2.1 %prep.1 = bf16[32,24,128]{2,1,0:T(8,128)(2,1)} custom-call(s32[1,32]{1,0:T(1,128)} %bitcast.50, bf16[1,32]{1,0:T(2,128)(2,1)} %bitcast.49, bf16[9,32,64]{2,1,0:T(8,128)(2,1)} %bitcast.45, bf16[9,32,64]{2,1,0:T(8,128)(2,1)} %bitcast.46), custom_call_target="tpu_custom_call" | custom-call | tf_op jit(solution)/shard_map/prep/pallas_call | solution.py:209
  2.7 0.0 copy-start.4
  2.7 17.8 %all-to-all-start = ((bf16[32,24,128]{2,1,0:T(8,128)(2,1)}), bf16[32,24,128]{2,1,0:T(8,128)(2,1)S(1)}, u32[]{:S(2)}, u32[]{:S(2)}) async-start(bf16[32,24,128]{2,1,0:T(8,128)(2,1)} %prep.1), calls=%async_computation | async-start | bytes 393216 | tf_op jit(solution)/shard_map/all_to_all | solution.py:205
  20.5 8.4 %all-to-all-done.in_ref = bf16[32,24,128]{2,1,0:T(8,128)(2,1)S(1)} async-done(((bf16[32,24,128]{2,1,0:T(8,128)(2,1)}), bf16[32,24,128]{2,1,0:T(8,128)(2,1)S(1)}, u32[]{:S(2)}, u32[]{:S(2)}) %all-to-all-start) | async-done | bytes 196640 | tf_op jit(solution)/shard_map/all_to_all | solution.py:205
  28.9 0.0 copy-start.1
  28.9 0.7 copy-done.1
  29.6 1.7 %sort.1 = (bf16[288,128]{1,0:T(8,128)(2,1)}, bf16[9,64,64]{2,1,0:T(8,128)(2,1)}, f32[64,128]{1,0:T(8,128)}) custom-call(bf16[32,24,128]{2,1,0:T(8,128)(2,1)} %copy-done.1), custom_call_target="tpu_custom_call" | custom-call | tf_op jit(solution)/shard_map/sort/pallas_call | solution.py:222
  31.3 43.7 %all-gather = bf16[2304,128]{1,0:T(8,128)(2,1)S(1)} all-gather(bf16[288,128]{1,0:T(8,128)(2,1)} %get-tuple-element.9), channel_id=2, replica_groups={{0,4,8,12,16,20,24,28},{1,5,9,13,17,21,25,29},{2,6,10,14,18,22,26,30},{..., dimensions={0}, use_global_device_ids=true | all-gather | bytes 663552 | tf_op jit(solution)/shard_map/all_gather | solution.py:236
  75.0 0.0 copy-start
  75.0 4.4 %collective-permute-start = (bf16[8,288,128]{2,1,0:T(8,128)(2,1)S(1)}, bf16[8,288,128]{2,1,0:T(8,128)(2,1)S(1)}, u32[]{:S(2)}, u32[]{:S(2)}) collective-permute-start(bf16[8,288,128]{2,1,0:T(8,128)(2,1)S(1)} %bitcast.36), channel_id=1, source_target_pairs={{0,31},{1,0},{2,1},{3,2},{4,3},{5,4},{6,5},{7,6},{8,7},{9,8},{10,9... | collective-permute-start | bytes 1769480 | tf_op jit(solution)/shard_map/ppermute | solution.py:239
  79.4 1.9 %collective-permute-start.3 = (bf16[8,288,128]{2,1,0:T(8,128)(2,1)S(1)}, bf16[8,288,128]{2,1,0:T(8,128)(2,1)S(1)}, u32[]{:S(2)}, u32[]{:S(2)}) collective-permute-start(bf16[8,288,128]{2,1,0:T(8,128)(2,1)S(1)} %bitcast.37), channel_id=1, source_target_pairs={{0,1},{1,2},{2,3},{3,4},{4,5},{5,6},{6,7},{7,8},{8,9},{9,10},{10,1... | collective-permute-start | bytes 1769480 | tf_op jit(solution)/shard_map/ppermute | solution.py:239
  81.4 2.1 %collective-permute-start.1 = (bf16[4,288,128]{2,1,0:T(8,128)(2,1)S(1)}, bf16[4,288,128]{2,1,0:T(8,128)(2,1)S(1)}, u32[]{:S(2)}, u32[]{:S(2)}) collective-permute-start(bf16[4,288,128]{2,1,0:T(8,128)(2,1)S(1)} %bitcast.43), channel_id=1, source_target_pairs={{0,2},{1,3},{2,4},{3,5},{4,6},{5,7},{6,8},{7,9},{8,10},{9,11},{10,... | collective-permute-start | bytes 884744 | tf_op jit(solution)/shard_map/ppermute | solution.py:239
  83.4 5.3 %collective-permute-start.2 = (bf16[4,288,128]{2,1,0:T(8,128)(2,1)S(1)}, bf16[4,288,128]{2,1,0:T(8,128)(2,1)S(1)}, u32[]{:S(2)}, u32[]{:S(2)}) collective-permute-start(bf16[4,288,128]{2,1,0:T(8,128)(2,1)S(1)} %bitcast.42), channel_id=1, source_target_pairs={{0,30},{1,31},{2,0},{3,1},{4,2},{5,3},{6,4},{7,5},{8,6},{9,7},{10,... | collective-permute-start | bytes 884744 | tf_op jit(solution)/shard_map/ppermute | solution.py:239
  88.8 0.0 copy-done.4
  88.8 0.1 bitcast_select_fusion.1
  88.9 0.9 pad_maximum_fusion.refs_1_.refs_3_
  89.7 0.0 copy-done
  89.7 3.5 %forward.1 = (bf16[9,64,512]{2,1,0:T(8,128)(2,1)}, f32[9,64,512]{2,1,0:T(8,128)}) custom-call(bf16[9,64,64]{2,1,0:T(8,128)(2,1)} %get-tuple-element.10.refs_0_, bf16[9,64,512]{2,1,0:T(8,128)(2,1)} %pad_maximum_fusion.refs_1_.refs_3_, bf16[9,512]{1,0:T(8,128)(2,1)} %bitcast.47), custom_call_target="tpu_custom_call" | custom-call | tf_op jit(solution)/shard_map/forward/pallas_call | solution.py:255
  93.2 6.1 %collective-permute-done.1.low_ref = bf16[4,288,128]{2,1,0:T(8,128)(2,1)S(1)} collective-permute-done((bf16[4,288,128]{2,1,0:T(8,128)(2,1)S(1)}, bf16[4,288,128]{2,1,0:T(8,128)(2,1)S(1)}, u32[]{:S(2)}, u32[]{:S(2)}) %collective-permute-start.1) | collective-permute-done | bytes 294944 | tf_op jit(solution)/shard_map/ppermute | solution.py:239
  99.3 0.0 copy-start.5
  99.3 0.6 collective-permute-done.2.high_ref
  99.9 0.0 copy-start.6
  99.9 0.0 collective-permute-done.next_ref
  99.9 0.0 collective-permute-done.3.prev_ref
  99.9 0.0 copy-start.3
  99.9 0.1 copy-done.5
  100.1 0.5 copy-done.6
  100.6 0.2 copy-done.2
  100.8 0.2 copy-done.3
  101.0 5.6 %project.1 = (bf16[9,64,512]{2,1,0:T(8,128)(2,1)}, f32[32,1,128]{2,1,0:T(1,128)}) custom-call(s32[1]{0:T(128)} %bitcast.3.turn_ref, bf16[8,288,128]{2,1,0:T(8,128)(2,1)} %bitcast.38, bf16[8,288,128]{2,1,0:T(8,128)(2,1)} %copy-done.2, bf16[4,288,128]{2,1,0:T(8,128)(2,1)} %copy-done.5, bf16[4,288,128]{2,1,0:T(8,128)(2,1)} %copy-done.6, ...), custom_call_target="tpu_custom_call" | custom-call | tf_op jit(solution)/shard_map/project/pallas_call | solution.py:267
  106.6 13.3 %all-to-all-start.1 = ((f32[32,1,128]{2,1,0:T(1,128)}), f32[32,1,128]{2,1,0:T(1,128)S(1)}, u32[]{:S(2)}, u32[]{:S(2)}) async-start(f32[32,1,128]{2,1,0:T(1,128)} %get-tuple-element.15), calls=%async_computation.1 | async-start | bytes 32768 | tf_op jit(solution)/shard_map/all_to_all | solution.py:281
  119.9 0.0 copy-done.7
  119.9 0.2 convert_reduce_fusion
  120.1 3.6 %back.1 = bf16[9,64,64]{2,1,0:T(8,128)(2,1)} custom-call(bf16[9,64,512]{2,1,0:T(8,128)(2,1)} %get-tuple-element.13.refs_0_, f32[9,64,512]{2,1,0:T(8,128)} %get-tuple-element.14.refs_1_, bf16[9,512]{1,0:T(8,128)(2,1)} %bitcast.48, bf16[9,64,512]{2,1,0:T(8,128)(2,1)} %pad_maximum_fusion.refs_1_.refs_3_), custom_call_target="tpu_custom_call" | custom-call | tf_op jit(solution)/shard_map/back/pallas_call | solution.py:283
  123.7 1.0 copy.27
  124.7 0.2 reshape.46
  124.9 16.2 %all-to-all-done.1 = f32[32,1,128]{2,1,0:T(1,128)S(1)} async-done(((f32[32,1,128]{2,1,0:T(1,128)}), f32[32,1,128]{2,1,0:T(1,128)S(1)}, u32[]{:S(2)}, u32[]{:S(2)}) %all-to-all-start.1) | async-done | bytes 16416 | tf_op jit(solution)/shard_map/all_to_all | solution.py:281
  141.0 0.1 reduce_sum.22
  141.1 0.1 convert_element_type.15
  141.2 0.1 copy.23
  141.3 0.1 fusion.1
  141.4 0.7 copy.24
  142.1 14.3 %all-to-all-start.2 = ((bf16[32,2,640]{2,1,0:T(2,128)(2,1)}), bf16[32,2,640]{2,1,0:T(2,128)(2,1)S(1)}, u32[]{:S(2)}, u32[]{:S(2)}) async-start(bf16[32,2,640]{2,1,0:T(2,128)(2,1)} %copy.24), calls=%async_computation.2 | async-start | bytes 163840 | tf_op jit(solution)/shard_map/all_to_all | solution.py:205
  156.3 7.4 %all-to-all-done.2 = bf16[32,2,640]{2,1,0:T(2,128)(2,1)S(1)} async-done(((bf16[32,2,640]{2,1,0:T(2,128)(2,1)}), bf16[32,2,640]{2,1,0:T(2,128)(2,1)S(1)}, u32[]{:S(2)}, u32[]{:S(2)}) %all-to-all-start.2) | async-done | bytes 81952 | tf_op jit(solution)/shard_map/all_to_all | solution.py:205
  163.8 0.2 convolution_convert_fusion
  164.0 0.7 slice_reduce_fusion
  164.7 0.1 reshape.48
  164.8 0.6 copy.25
  (6 shorter events, 0.1 us)
Async XLA Ops:
  2.7 86.1 %copy-start.4 = (bf16[1,3,3,32,512]{4,3,2,1,0:T(8,128)(2,1)S(1)}, bf16[1,3,3,32,512]{4,3,2,1,0:T(8,128)(2,1)}, u32[]{:S(2)}) copy-start(bf16[1,3,3,32,512]{4,3,2,1,0:T(8,128)(2,1)} %param.11) | copy-start | bytes 884740
  2.7 26.2 %all-to-all-start = ((bf16[32,24,128]{2,1,0:T(8,128)(2,1)}), bf16[32,24,128]{2,1,0:T(8,128)(2,1)S(1)}, u32[]{:S(2)}, u32[]{:S(2)}) async-start(bf16[32,24,128]{2,1,0:T(8,128)(2,1)} %prep.1), calls=%async_computation | async-start | bytes 393216 | tf_op jit(solution)/shard_map/all_to_all | solution.py:205
  28.9 0.7 copy-start.1
  75.0 14.7 %copy-start = (bf16[2304,128]{1,0:T(8,128)(2,1)}, bf16[2304,128]{1,0:T(8,128)(2,1)S(1)}, u32[]{:S(2)}) copy-start(bf16[2304,128]{1,0:T(8,128)(2,1)S(1)} %all-gather) | copy-start | bytes 1769476
  75.0 24.9 %collective-permute-start = (bf16[8,288,128]{2,1,0:T(8,128)(2,1)S(1)}, bf16[8,288,128]{2,1,0:T(8,128)(2,1)S(1)}, u32[]{:S(2)}, u32[]{:S(2)}) collective-permute-start(bf16[8,288,128]{2,1,0:T(8,128)(2,1)S(1)} %bitcast.36), channel_id=1, source_target_pairs={{0,31},{1,0},{2,1},{3,2},{4,3},{5,4},{6,5},{7,6},{8,7},{9,8},{10,9... | collective-permute-start | bytes 1769480 | tf_op jit(solution)/shard_map/ppermute | solution.py:239
  79.4 20.5 %collective-permute-start.3 = (bf16[8,288,128]{2,1,0:T(8,128)(2,1)S(1)}, bf16[8,288,128]{2,1,0:T(8,128)(2,1)S(1)}, u32[]{:S(2)}, u32[]{:S(2)}) collective-permute-start(bf16[8,288,128]{2,1,0:T(8,128)(2,1)S(1)} %bitcast.37), channel_id=1, source_target_pairs={{0,1},{1,2},{2,3},{3,4},{4,5},{5,6},{6,7},{7,8},{8,9},{9,10},{10,1... | collective-permute-start | bytes 1769480 | tf_op jit(solution)/shard_map/ppermute | solution.py:239
  81.4 18.0 %collective-permute-start.1 = (bf16[4,288,128]{2,1,0:T(8,128)(2,1)S(1)}, bf16[4,288,128]{2,1,0:T(8,128)(2,1)S(1)}, u32[]{:S(2)}, u32[]{:S(2)}) collective-permute-start(bf16[4,288,128]{2,1,0:T(8,128)(2,1)S(1)} %bitcast.43), channel_id=1, source_target_pairs={{0,2},{1,3},{2,4},{3,5},{4,6},{5,7},{6,8},{7,9},{8,10},{9,11},{10,... | collective-permute-start | bytes 884744 | tf_op jit(solution)/shard_map/ppermute | solution.py:239
  83.4 16.5 %collective-permute-start.2 = (bf16[4,288,128]{2,1,0:T(8,128)(2,1)S(1)}, bf16[4,288,128]{2,1,0:T(8,128)(2,1)S(1)}, u32[]{:S(2)}, u32[]{:S(2)}) collective-permute-start(bf16[4,288,128]{2,1,0:T(8,128)(2,1)S(1)} %bitcast.42), channel_id=1, source_target_pairs={{0,30},{1,31},{2,0},{3,1},{4,2},{5,3},{6,4},{7,5},{8,6},{9,7},{10,... | collective-permute-start | bytes 884744 | tf_op jit(solution)/shard_map/ppermute | solution.py:239
  99.3 0.7 copy-start.5
  99.9 0.7 copy-start.6
  99.9 0.9 copy-start.2
  99.9 1.1 copy-start.3
  101.0 18.9 %copy-start.7 = (s32[32,1]{0,1:T(1,128)S(1)}, s32[32,1]{0,1:T(1,128)}, u32[]{:S(2)}) copy-start(s32[32,1]{0,1:T(1,128)} %param.10) | copy-start | bytes 388
  106.6 34.5 %all-to-all-start.1 = ((f32[32,1,128]{2,1,0:T(1,128)}), f32[32,1,128]{2,1,0:T(1,128)S(1)}, u32[]{:S(2)}, u32[]{:S(2)}) async-start(f32[32,1,128]{2,1,0:T(1,128)} %get-tuple-element.15), calls=%async_computation.1 | async-start | bytes 32768 | tf_op jit(solution)/shard_map/all_to_all | solution.py:281
  142.1 21.7 %all-to-all-start.2 = ((bf16[32,2,640]{2,1,0:T(2,128)(2,1)}), bf16[32,2,640]{2,1,0:T(2,128)(2,1)S(1)}, u32[]{:S(2)}, u32[]{:S(2)}) async-start(bf16[32,2,640]{2,1,0:T(2,128)(2,1)} %copy.24), calls=%async_computation.2 | async-start | bytes 163840 | tf_op jit(solution)/shard_map/all_to_all | solution.py:205

commit v4 on v3

--- a/solution.py
+++ b/solution.py
@@ -90,21 +90,11 @@
             h_two_ref[pos, :, span] = total.astype(jnp.bfloat16)
 
 
-def project_kernel(
-    turn_ref, own_ref, next_ref, low_ref, high_ref, prev_ref, weight_ref, h_two_ref, gate_ref,
-    d_two_ref, part_ref, left_ref, sums_ref,
-):
+def early_kernel(turn_ref, own_ref, next_ref, prev_ref, weight_ref, upper_ref, late_ref, left_ref):
     steps, rows, lanes = own_ref.shape
     half = lanes // 2
-    tokens, slots, hidden = d_two_ref.shape
-    own = slots // 2
-
-    def block(kind, step):
-        if kind == 2:
-            ref, step = (low_ref, step) if step < steps // 2 else (high_ref, step - steps // 2)
-        else:
-            ref = (own_ref, next_ref, None, prev_ref)[kind]
-        return ref[step]
+    hidden = weight_ref.shape[0]
+    blank = jnp.zeros((rows, half), jnp.bfloat16)
 
     for turn in range(4):
 
@@ -112,45 +102,81 @@
         def _():
             for step in range(steps):
                 for pair in range(2):
-                    first = block((2 * pair - turn) % 4, step)
-                    second = block((2 * pair + 1 - turn) % 4, step)
+                    kinds = [(2 * pair + side - turn) % 4 for side in range(2)]
+                    refs = [(own_ref, next_ref, None, prev_ref)[kind] for kind in kinds]
+                    blocks = [None if ref is None else ref[step] for ref in refs]
                     start = (2 * step + pair) * lanes
-                    span = slice(start, start + lanes)
-                    left_ref[:rows, span] = jnp.concatenate(
-                        [first[:, :half], second[:, :half]], axis=1
+                    for group in range(2):
+                        part = slice(group * half, (group + 1) * half)
+                        left_ref[group * rows : (group + 1) * rows, start : start + lanes] = (
+                            jnp.concatenate(
+                                [blank if x is None else x[:, part] for x in blocks], axis=1
+                            )
+                        )
+            for step in range(0, steps, 2):
+                cuts = []
+                for inner in range(2):
+                    start = (4 * (step + inner) + (turn + 2) % 4) * half
+                    cuts.append(weight_ref[:, start : start + half])
+                late_ref[:, step * half : (step + 2) * half] = jnp.concatenate(cuts, axis=1)
+
+    wide = 256
+    for start in range(0, hidden, wide):
+        upper_ref[:, start : start + wide] = lax.dot_general(
+            left_ref[...],
+            weight_ref[start : start + wide, :],
+            (((1,), (1,)), ((), ())),
+            preferred_element_type=jnp.float32,
+        )
+
+
+def project_kernel(
+    low_ref, high_ref, late_ref, upper_ref, h_two_ref, gate_ref, d_two_ref, part_ref,
+    left_ref, sums_ref,
+):
+    steps, rows, lanes = low_ref.shape
+    half = lanes // 2
+    tokens, slots, wide = d_two_ref.shape
+    own = slots // 2
+
+    @pl.when(pl.program_id(0) == 0)
+    def _():
+        sums_ref[...] = jnp.zeros(sums_ref.shape, jnp.float32)
+        for place, ref in enumerate((low_ref, high_ref)):
+            for step in range(0, steps, 2):
+                start = (place * steps + step) * half
+                for group in range(2):
+                    part = slice(group * half, (group + 1) * half)
+                    left_ref[group * rows : (group + 1) * rows, start : start + lanes] = (
+                        jnp.concatenate([ref[step][:, part], ref[step + 1][:, part]], axis=1)
                     )
-                    left_ref[rows:, span] = jnp.concatenate(
-                        [first[:, half:], second[:, half:]], axis=1
-                    )
-
-    wide = 256
-    sums_ref[...] = jnp.zeros(sums_ref.shape, jnp.float32)
+
+    rest = lax.dot_general(
+        left_ref[...], late_ref[...], (((1,), (1,)), ((), ())), preferred_element_type=jnp.float32
+    )
     for group in range(2):
         keep = slice(group * own, (group + 1) * own)
         scale = gate_ref[keep, :][:, :1]
-        total = jnp.zeros((own, 128), jnp.float32)
-        for start in range(0, hidden, wide):
-            upper = lax.dot_general(
-                left_ref[group * rows : (group + 1) * rows, :],
-                weight_ref[start : start + wide, :],
-                (((1,), (1,)), ((), ())),
-                preferred_element_type=jnp.float32,
-            )
-            for pos in range(tokens):
-                piece = upper[pos * own : (pos + 1) * own, :]
-                d_two_ref[pos, keep, start : start + wide] = (piece * scale).astype(jnp.bfloat16)
-                prod = h_two_ref[pos, keep, start : start + wide].astype(jnp.float32) * piece
-                for lane in range(0, wide, 128):
-                    total = total + prod[:, lane : lane + 128]
+        total = sums_ref[keep, :]
+        for pos in range(tokens):
+            row = group * rows + pos * own
+            piece = upper_ref[row : row + own, :] + rest[row : row + own, :]
+            d_two_ref[pos, keep, :] = (piece * scale).astype(jnp.bfloat16)
+            prod = h_two_ref[pos, keep, :].astype(jnp.float32) * piece
+            for lane in range(0, wide, 128):
+                total = total + prod[:, lane : lane + 128]
         sums_ref[keep, :] = total
-    row = lax.dot_general(
-        jnp.ones((8, 128), jnp.float32),
-        sums_ref[...],
-        (((1,), (1,)), ((), ())),
-        preferred_element_type=jnp.float32,
-        precision=lax.Precision.HIGHEST,
-    )[:1]
-    part_ref[...] = jnp.broadcast_to(row[None], part_ref.shape)
+
+    @pl.when(pl.program_id(0) == pl.num_programs(0) - 1)
+    def _():
+        row = lax.dot_general(
+            jnp.ones((8, 128), jnp.float32),
+            sums_ref[...],
+            (((1,), (1,)), ((), ())),
+            preferred_element_type=jnp.float32,
+            precision=lax.Precision.HIGHEST,
+        )[:1]
+        part_ref[...] = jnp.broadcast_to(row[None], part_ref.shape)
 
 
 def back_kernel(d_two_ref, slope_ref, taps_ref, kernel_ref, d_in_ref, d_one_ref, *, side):
@@ -264,20 +290,45 @@
         name="forward",
     )(inputs, kernel, taps)
 
+    features = w_out.shape[2]
+    upper, late = pl.pallas_call(
+        early_kernel,
+        out_shape=(
+            jax.ShapeDtypeStruct((tokens * slots, hidden), jnp.float32),
+            jax.ShapeDtypeStruct((hidden, features // 4), jnp.bfloat16),
+        ),
+        in_specs=[pl.BlockSpec(memory_space=pltpu.SMEM)] + vmem(4),
+        out_specs=tuple(vmem(2)),
+        scratch_shapes=[pltpu.VMEM((tokens * slots, features), jnp.bfloat16)],
+        name="early",
+    )(turn, own, following, prev, w_out[0])
+    wide = 256
+    whole = lambda shape: pl.BlockSpec(shape, lambda i: (0,) * len(shape))
     d_two, part = pl.pallas_call(
         project_kernel,
+        grid=(hidden // wide,),
         out_shape=(
             jax.ShapeDtypeStruct((tokens, slots, hidden), jnp.bfloat16),
             jax.ShapeDtypeStruct((chans, 1, 128), jnp.float32),
         ),
-        in_specs=[pl.BlockSpec(memory_space=pltpu.SMEM)] + vmem(8),
-        out_specs=tuple(vmem(2)),
+        in_specs=[
+            whole(low.shape),
+            whole(high.shape),
+            pl.BlockSpec((wide, features // 4), lambda i: (i, 0)),
+            pl.BlockSpec((tokens * slots, wide), lambda i: (0, i)),
+            pl.BlockSpec((tokens, slots, wide), lambda i: (0, 0, i)),
+            whole(gates.shape),
+        ],
+        out_specs=(
+            pl.BlockSpec((tokens, slots, wide), lambda i: (0, 0, i)),
+            whole((chans, 1, 128)),
+        ),
         scratch_shapes=[
-            pltpu.VMEM((tokens * slots, w_out.shape[2]), jnp.bfloat16),
+            pltpu.VMEM((tokens * slots, features // 4), jnp.bfloat16),
             pltpu.VMEM((128, 128), jnp.float32),
         ],
         name="project",
-    )(turn, own, following, low, high, prev, w_out[0], h_two, gates)
+    )(low, high, late, upper, h_two, gates)
     parts = lax.all_to_all(part, "chan", split_axis=0, concat_axis=0, tiled=True)
     gate_grad = jnp.sum(parts[:, 0], axis=0)[:slots].astype(jnp.bfloat16)
     d_input = pl.pallas_call(

time: 166 us -> 166 us (level)
  waiting for transfers between devices: 38.6 us -> 32.3 us
  Pallas kernels: 16.4 us -> 19.7 us
  starting transfers between devices: 59 us -> 61.3 us
    ppermute x4, waiting for transfers between devices: 6.65 us -> 0.29 us  [shift(): lax.ppermute(array, 'chan', [(c, (c + by) % chans) for c in range(chans)])]
    pallas_call x1 -> x2, Pallas kernels: 5.56 us -> 8.86 us  [the longest x1 5.35 us: on_device(): pl.pallas_call(early_kernel, out_shape=(jax.ShapeDtypeStruct((tokens * sl...]
    all_to_all x2, starting transfers between devices: 32 us -> 34.3 us  [exchange(): lax.all_to_all(array, 'expert', split_axis=0, concat_axis=0, tiled=True)]
  transfers between devices with their start and end apart: 7 -> 7, of which waited for: 5 -> 4; matrix products, arithmetic and copies ran while one was open for 1% -> 1% of each run, Pallas kernels for 4% -> 8%
where the time goes in v4:
time: 166 us; the launch traced here: 165 us
  starting transfers between devices  61.3 us (37%)
  blocking collectives  43.7 us (26%)
  waiting for transfers between devices  32.3 us (19%)
  Pallas kernels  19.7 us (12%)
  local copies, waits for them, and re-layouts  6.06 us (4%)
    all_gather x1, blocking collectives, on_device(): own = lax.all_gather(packed, 'chan', axis=0, axis_index_groups=families)  43.7 us
    all_to_all x2, starting transfers between devices, exchange(): lax.all_to_all(array, 'expert', split_axis=0, concat_axis=0, tiled=True)  34.3 us
    all_to_all x1, waiting for transfers between devices, on_device(): lax.all_to_all(part, 'chan', split_axis=0, concat_axis=0, tiled=True)  16.2 us
    all_to_all x2, waiting for transfers between devices, exchange(): lax.all_to_all(array, 'expert', split_axis=0, concat_axis=0, tiled=True)  15.8 us
    ppermute x4, starting transfers between devices, shift(): lax.ppermute(array, 'chan', [(c, (c + by) % chans) for c in range(chans)])  13.7 us
    all_to_all x1, starting transfers between devices, on_device(): lax.all_to_all(part, 'chan', split_axis=0, concat_axis=0, tiled=True)  13.3 us
    pallas_call x1, Pallas kernels, on_device(): pl.pallas_call(early_kernel, out_shape=(jax.ShapeDtypeStruct((tokens * sl...  5.35 us
    pallas_call x1, Pallas kernels, on_device(): pl.pallas_call(lambda *refs: back_kernel(*refs, side=side), out_shape=jax...  3.59 us
  transfers between devices with their start and end apart: 7, of which 4 were waited for; matrix products, arithmetic and copies ran while one was open for 1% of the time, Pallas kernels for 8%

profile of v4, /device:TPU:1, one launch (start us, length us, event | category | flops | bytes accessed | tf_op | source)
XLA Modules:
  0.0 165.4 jit_solution(4889405004597764006)
XLA Ops:
  0.6 2.0 %prep.1 = bf16[32,24,128]{2,1,0:T(8,128)(2,1)} custom-call(s32[1,32]{1,0:T(1,128)} %bitcast.50, bf16[1,32]{1,0:T(2,128)(2,1)} %bitcast.49, bf16[9,32,64]{2,1,0:T(8,128)(2,1)} %bitcast.45, bf16[9,32,64]{2,1,0:T(8,128)(2,1)} %bitcast.46), custom_call_target="tpu_custom_call" | custom-call | tf_op jit(solution)/shard_map/prep/pallas_call | solution.py:235
  2.7 17.8 %all-to-all-start = ((bf16[32,24,128]{2,1,0:T(8,128)(2,1)}), bf16[32,24,128]{2,1,0:T(8,128)(2,1)S(1)}, u32[]{:S(2)}, u32[]{:S(2)}) async-start(bf16[32,24,128]{2,1,0:T(8,128)(2,1)} %prep.1), calls=%async_computation | async-start | bytes 393216 | tf_op jit(solution)/shard_map/all_to_all | solution.py:231
  20.5 8.4 %all-to-all-done.in_ref = bf16[32,24,128]{2,1,0:T(8,128)(2,1)S(1)} async-done(((bf16[32,24,128]{2,1,0:T(8,128)(2,1)}), bf16[32,24,128]{2,1,0:T(8,128)(2,1)S(1)}, u32[]{:S(2)}, u32[]{:S(2)}) %all-to-all-start) | async-done | bytes 196640 | tf_op jit(solution)/shard_map/all_to_all | solution.py:231
  28.9 0.0 copy-start.1
  28.9 0.7 copy-done.1
  29.5 1.7 %sort.1 = (bf16[288,128]{1,0:T(8,128)(2,1)}, bf16[9,64,64]{2,1,0:T(8,128)(2,1)}, f32[64,128]{1,0:T(8,128)}) custom-call(bf16[32,24,128]{2,1,0:T(8,128)(2,1)} %copy-done.1), custom_call_target="tpu_custom_call" | custom-call | tf_op jit(solution)/shard_map/sort/pallas_call | solution.py:248
  31.3 43.7 %all-gather = bf16[2304,128]{1,0:T(8,128)(2,1)S(1)} all-gather(bf16[288,128]{1,0:T(8,128)(2,1)} %get-tuple-element.11), channel_id=2, replica_groups={{0,4,8,12,16,20,24,28},{1,5,9,13,17,21,25,29},{2,6,10,14,18,22,26,30},{..., dimensions={0}, use_global_device_ids=true | all-gather | bytes 663552 | tf_op jit(solution)/shard_map/all_gather | solution.py:262
  75.0 0.0 copy-start
  75.0 4.4 %collective-permute-start.2 = (bf16[8,288,128]{2,1,0:T(8,128)(2,1)S(1)}, bf16[8,288,128]{2,1,0:T(8,128)(2,1)S(1)}, u32[]{:S(2)}, u32[]{:S(2)}) collective-permute-start(bf16[8,288,128]{2,1,0:T(8,128)(2,1)S(1)} %bitcast.36), channel_id=1, source_target_pairs={{0,31},{1,0},{2,1},{3,2},{4,3},{5,4},{6,5},{7,6},{8,7},{9,8},{10,9... | collective-permute-start | bytes 1769480 | tf_op jit(solution)/shard_map/ppermute | solution.py:265
  79.4 1.9 %collective-permute-start.3 = (bf16[8,288,128]{2,1,0:T(8,128)(2,1)S(1)}, bf16[8,288,128]{2,1,0:T(8,128)(2,1)S(1)}, u32[]{:S(2)}, u32[]{:S(2)}) collective-permute-start(bf16[8,288,128]{2,1,0:T(8,128)(2,1)S(1)} %bitcast.37), channel_id=1, source_target_pairs={{0,1},{1,2},{2,3},{3,4},{4,5},{5,6},{6,7},{7,8},{8,9},{9,10},{10,1... | collective-permute-start | bytes 1769480 | tf_op jit(solution)/shard_map/ppermute | solution.py:265
  81.4 2.1 %collective-permute-start = (bf16[4,288,128]{2,1,0:T(8,128)(2,1)S(1)}, bf16[4,288,128]{2,1,0:T(8,128)(2,1)S(1)}, u32[]{:S(2)}, u32[]{:S(2)}) collective-permute-start(bf16[4,288,128]{2,1,0:T(8,128)(2,1)S(1)} %bitcast.43), channel_id=1, source_target_pairs={{0,2},{1,3},{2,4},{3,5},{4,6},{5,7},{6,8},{7,9},{8,10},{9,11},{10,... | collective-permute-start | bytes 884744 | tf_op jit(solution)/shard_map/ppermute | solution.py:265
  83.4 5.3 %collective-permute-start.1 = (bf16[4,288,128]{2,1,0:T(8,128)(2,1)S(1)}, bf16[4,288,128]{2,1,0:T(8,128)(2,1)S(1)}, u32[]{:S(2)}, u32[]{:S(2)}) collective-permute-start(bf16[4,288,128]{2,1,0:T(8,128)(2,1)S(1)} %bitcast.42), channel_id=1, source_target_pairs={{0,30},{1,31},{2,0},{3,1},{4,2},{5,3},{6,4},{7,5},{8,6},{9,7},{10,... | collective-permute-start | bytes 884744 | tf_op jit(solution)/shard_map/ppermute | solution.py:265
  88.8 0.0 copy-done.4
  88.8 0.1 bitcast_select_fusion.1
  88.9 0.9 pad_maximum_fusion.refs_1_.refs_3_
  89.7 0.0 copy-done
  89.7 3.5 %forward.1 = (bf16[9,64,512]{2,1,0:T(8,128)(2,1)}, f32[9,64,512]{2,1,0:T(8,128)}) custom-call(bf16[9,64,64]{2,1,0:T(8,128)(2,1)} %get-tuple-element.14.refs_0_, bf16[9,64,512]{2,1,0:T(8,128)(2,1)} %pad_maximum_fusion.refs_1_.refs_3_, bf16[9,512]{1,0:T(8,128)(2,1)} %bitcast.47), custom_call_target="tpu_custom_call" | custom-call | tf_op jit(solution)/shard_map/forward/pallas_call | solution.py:281
  93.2 0.0 collective-permute-done.2.next_ref
  93.2 0.0 copy-start.2
  93.2 0.0 collective-permute-done.3.prev_ref
  93.2 0.0 copy-start.3
  93.2 0.8 copy-done.2
  94.1 0.2 copy-done.3
  94.2 5.4 %early.1 = (f32[576,512]{1,0:T(8,128)}, bf16[512,512]{1,0:T(8,128)(2,1)}) custom-call(s32[1]{0:T(128)} %bitcast.11.turn_ref, bf16[8,288,128]{2,1,0:T(8,128)(2,1)} %bitcast.38, bf16[8,288,128]{2,1,0:T(8,128)(2,1)} %copy-done.2, bf16[8,288,128]{2,1,0:T(8,128)(2,1)} %copy-done.3, bf16[512,2048]{1,0:T(8,128)(2,1)} %bitcast.39), custom_call_target="tpu_custom_call" | custom-call | tf_op jit(solution)/shard_map/early/pallas_call | solution.py:294
  99.6 0.0 collective-permute-done.low_ref
  99.6 0.0 copy-start.5
  99.6 0.3 collective-permute-done.1.high_ref
  99.9 0.4 copy-done.5
  100.3 0.3 copy-done.6
  100.6 3.5 %project.1 = (bf16[9,64,512]{2,1,0:T(8,128)(2,1)}, f32[32,1,128]{2,1,0:T(1,128)}) custom-call(bf16[4,288,128]{2,1,0:T(8,128)(2,1)} %copy-done.5, bf16[4,288,128]{2,1,0:T(8,128)(2,1)} %copy-done.6, bf16[512,512]{1,0:T(8,128)(2,1)} %get-tuple-element.12.late_ref, f32[576,512]{1,0:T(8,128)} %get-tuple-element.13.upper_ref, ...), custom_call_target="tpu_custom_call" | custom-call | tf_op jit(solution)/shard_map/project/pallas_call | solution.py:307
  104.1 13.3 %all-to-all-start.1 = ((f32[32,1,128]{2,1,0:T(1,128)}), f32[32,1,128]{2,1,0:T(1,128)S(1)}, u32[]{:S(2)}, u32[]{:S(2)}) async-start(f32[32,1,128]{2,1,0:T(1,128)} %get-tuple-element.19), calls=%async_computation.1 | async-start | bytes 32768 | tf_op jit(solution)/shard_map/all_to_all | solution.py:332
  117.4 0.0 copy-done.7
  117.5 0.2 convert_reduce_fusion
  117.6 3.6 %back.1 = bf16[9,64,64]{2,1,0:T(8,128)(2,1)} custom-call(bf16[9,64,512]{2,1,0:T(8,128)(2,1)} %get-tuple-element.17.refs_0_, f32[9,64,512]{2,1,0:T(8,128)} %get-tuple-element.18.refs_1_, bf16[9,512]{1,0:T(8,128)(2,1)} %bitcast.48, bf16[9,64,512]{2,1,0:T(8,128)(2,1)} %pad_maximum_fusion.refs_1_.refs_3_), custom_call_target="tpu_custom_call" | custom-call | tf_op jit(solution)/shard_map/back/pallas_call | solution.py:334
  121.2 1.0 copy.27
  122.2 0.2 reshape.46
  122.4 16.2 %all-to-all-done.1 = f32[32,1,128]{2,1,0:T(1,128)S(1)} async-done(((f32[32,1,128]{2,1,0:T(1,128)}), f32[32,1,128]{2,1,0:T(1,128)S(1)}, u32[]{:S(2)}, u32[]{:S(2)}) %all-to-all-start.1) | async-done | bytes 16416 | tf_op jit(solution)/shard_map/all_to_all | solution.py:332
  138.6 0.1 reduce_sum.22
  138.7 0.1 convert_element_type.15
  138.8 0.1 copy.23
  138.9 0.1 fusion.1
  139.0 0.7 copy.24
  139.7 16.6 %all-to-all-start.2 = ((bf16[32,2,640]{2,1,0:T(2,128)(2,1)}), bf16[32,2,640]{2,1,0:T(2,128)(2,1)S(1)}, u32[]{:S(2)}, u32[]{:S(2)}) async-start(bf16[32,2,640]{2,1,0:T(2,128)(2,1)} %copy.24), calls=%async_computation.2 | async-start | bytes 163840 | tf_op jit(solution)/shard_map/all_to_all | solution.py:231
  156.3 7.4 %all-to-all-done.2 = bf16[32,2,640]{2,1,0:T(2,128)(2,1)S(1)} async-done(((bf16[32,2,640]{2,1,0:T(2,128)(2,1)}), bf16[32,2,640]{2,1,0:T(2,128)(2,1)S(1)}, u32[]{:S(2)}, u32[]{:S(2)}) %all-to-all-start.2) | async-done | bytes 81952 | tf_op jit(solution)/shard_map/all_to_all | solution.py:231
  163.7 0.2 convolution_convert_fusion
  163.9 0.7 slice_reduce_fusion
  164.6 0.1 reshape.48
  164.7 0.6 copy.25
  (7 shorter events, 0.1 us)
Async XLA Ops:
  2.7 86.1 %copy-start.4 = (bf16[1,3,3,32,512]{4,3,2,1,0:T(8,128)(2,1)S(1)}, bf16[1,3,3,32,512]{4,3,2,1,0:T(8,128)(2,1)}, u32[]{:S(2)}) copy-start(bf16[1,3,3,32,512]{4,3,2,1,0:T(8,128)(2,1)} %param.11) | copy-start | bytes 884740
  2.7 26.2 %all-to-all-start = ((bf16[32,24,128]{2,1,0:T(8,128)(2,1)}), bf16[32,24,128]{2,1,0:T(8,128)(2,1)S(1)}, u32[]{:S(2)}, u32[]{:S(2)}) async-start(bf16[32,24,128]{2,1,0:T(8,128)(2,1)} %prep.1), calls=%async_computation | async-start | bytes 393216 | tf_op jit(solution)/shard_map/all_to_all | solution.py:231
  28.9 0.7 copy-start.1
  75.0 14.7 %copy-start = (bf16[2304,128]{1,0:T(8,128)(2,1)}, bf16[2304,128]{1,0:T(8,128)(2,1)S(1)}, u32[]{:S(2)}) copy-start(bf16[2304,128]{1,0:T(8,128)(2,1)S(1)} %all-gather) | copy-start | bytes 1769476
  75.0 18.2 %collective-permute-start.2 = (bf16[8,288,128]{2,1,0:T(8,128)(2,1)S(1)}, bf16[8,288,128]{2,1,0:T(8,128)(2,1)S(1)}, u32[]{:S(2)}, u32[]{:S(2)}) collective-permute-start(bf16[8,288,128]{2,1,0:T(8,128)(2,1)S(1)} %bitcast.36), channel_id=1, source_target_pairs={{0,31},{1,0},{2,1},{3,2},{4,3},{5,4},{6,5},{7,6},{8,7},{9,8},{10,9... | collective-permute-start | bytes 1769480 | tf_op jit(solution)/shard_map/ppermute | solution.py:265
  79.4 13.8 %collective-permute-start.3 = (bf16[8,288,128]{2,1,0:T(8,128)(2,1)S(1)}, bf16[8,288,128]{2,1,0:T(8,128)(2,1)S(1)}, u32[]{:S(2)}, u32[]{:S(2)}) collective-permute-start(bf16[8,288,128]{2,1,0:T(8,128)(2,1)S(1)} %bitcast.37), channel_id=1, source_target_pairs={{0,1},{1,2},{2,3},{3,4},{4,5},{5,6},{6,7},{7,8},{8,9},{9,10},{10,1... | collective-permute-start | bytes 1769480 | tf_op jit(solution)/shard_map/ppermute | solution.py:265
  81.4 18.2 %collective-permute-start = (bf16[4,288,128]{2,1,0:T(8,128)(2,1)S(1)}, bf16[4,288,128]{2,1,0:T(8,128)(2,1)S(1)}, u32[]{:S(2)}, u32[]{:S(2)}) collective-permute-start(bf16[4,288,128]{2,1,0:T(8,128)(2,1)S(1)} %bitcast.43), channel_id=1, source_target_pairs={{0,2},{1,3},{2,4},{3,5},{4,6},{5,7},{6,8},{7,9},{8,10},{9,11},{10,... | collective-permute-start | bytes 884744 | tf_op jit(solution)/shard_map/ppermute | solution.py:265
  83.4 16.5 %collective-permute-start.1 = (bf16[4,288,128]{2,1,0:T(8,128)(2,1)S(1)}, bf16[4,288,128]{2,1,0:T(8,128)(2,1)S(1)}, u32[]{:S(2)}, u32[]{:S(2)}) collective-permute-start(bf16[4,288,128]{2,1,0:T(8,128)(2,1)S(1)} %bitcast.42), channel_id=1, source_target_pairs={{0,30},{1,31},{2,0},{3,1},{4,2},{5,3},{6,4},{7,5},{8,6},{9,7},{10,... | collective-permute-start | bytes 884744 | tf_op jit(solution)/shard_map/ppermute | solution.py:265
  93.2 0.8 copy-start.2
  93.2 1.0 copy-start.3
  99.6 0.7 copy-start.5
  99.9 0.7 copy-start.6
  100.6 16.8 %copy-start.7 = (s32[32,1]{0,1:T(1,128)S(1)}, s32[32,1]{0,1:T(1,128)}, u32[]{:S(2)}) copy-start(s32[32,1]{0,1:T(1,128)} %param.10) | copy-start | bytes 388
  104.1 34.5 %all-to-all-start.1 = ((f32[32,1,128]{2,1,0:T(1,128)}), f32[32,1,128]{2,1,0:T(1,128)S(1)}, u32[]{:S(2)}, u32[]{:S(2)}) async-start(f32[32,1,128]{2,1,0:T(1,128)} %get-tuple-element.19), calls=%async_computation.1 | async-start | bytes 32768 | tf_op jit(solution)/shard_map/all_to_all | solution.py:332
  139.7 24.0 %all-to-all-start.2 = ((bf16[32,2,640]{2,1,0:T(2,128)(2,1)}), bf16[32,2,640]{2,1,0:T(2,128)(2,1)S(1)}, u32[]{:S(2)}, u32[]{:S(2)}) async-start(bf16[32,2,640]{2,1,0:T(2,128)(2,1)} %copy.24), calls=%async_computation.2 | async-start | bytes 163840 | tf_op jit(solution)/shard_map/all_to_all | solution.py:231

commit v5 on v4

--- a/solution.py
+++ b/solution.py
@@ -4,6 +4,7 @@
 from jax.experimental import pallas as pl
 from jax.experimental.pallas import tpu as pltpu
 from jax.sharding import PartitionSpec as P
+
 
 CAP = 2
 
@@ -207,6 +208,10 @@
         d_in_ref[pos] = total.astype(jnp.bfloat16)
 
 
+def near_by(array):
+    return pltpu.with_memory_space_constraint(array, pltpu.VMEM)
+
+
 def vmem(count):
     return [pl.BlockSpec(memory_space=pltpu.VMEM) for _ in range(count)]
 
@@ -237,6 +242,7 @@
         out_shape=jax.ShapeDtypeStruct((sections, lines, CAP * feat), jnp.bfloat16),
         in_specs=vmem(4),
         out_specs=vmem(1)[0],
+        compiler_params=pltpu.CompilerParams(vmem_limit_bytes=24 << 20),
         name="prep",
     )(
         expert_id.reshape(1, owned),
@@ -254,8 +260,9 @@
         ),
         in_specs=vmem(1),
         out_specs=tuple(vmem(3)),
+        compiler_params=pltpu.CompilerParams(vmem_limit_bytes=24 << 20),
         name="sort",
-    )(arrived)
+    )(near_by(arrived))
     chans = lax.axis_size("chan")
     steps = chans // 4
     families = [[4 * step + kind for step in range(steps)] for kind in range(4)]
@@ -264,10 +271,10 @@
     def shift(array, by):
         return lax.ppermute(array, "chan", [(c, (c + by) % chans) for c in range(chans)])
 
-    low = shift(own[: steps // 2], 2)
-    high = shift(own[steps // 2 :], -2)
     prev = shift(own, 1)
     following = shift(own, -1)
+    low = shift(prev[: steps // 2], 1)
+    high = shift(following[steps // 2 :], -1)
     turn = (lax.axis_index("chan") % 4).astype(jnp.int32).reshape(1)
 
     taps = w_depth[0]
@@ -287,6 +294,7 @@
         in_specs=vmem(3),
         out_specs=tuple(vmem(2)),
         scratch_shapes=[pltpu.VMEM((tokens, slots, hidden), jnp.float32)],
+        compiler_params=pltpu.CompilerParams(vmem_limit_bytes=24 << 20),
         name="forward",
     )(inputs, kernel, taps)
 
@@ -300,8 +308,9 @@
         in_specs=[pl.BlockSpec(memory_space=pltpu.SMEM)] + vmem(4),
         out_specs=tuple(vmem(2)),
         scratch_shapes=[pltpu.VMEM((tokens * slots, features), jnp.bfloat16)],
+        compiler_params=pltpu.CompilerParams(vmem_limit_bytes=24 << 20),
         name="early",
-    )(turn, own, following, prev, w_out[0])
+    )(turn, near_by(own), near_by(following), near_by(prev), near_by(w_out[0]))
     wide = 256
     whole = lambda shape: pl.BlockSpec(shape, lambda i: (0,) * len(shape))
     d_two, part = pl.pallas_call(
@@ -327,8 +336,9 @@
             pltpu.VMEM((tokens * slots, features // 4), jnp.bfloat16),
             pltpu.VMEM((128, 128), jnp.float32),
         ],
+        compiler_params=pltpu.CompilerParams(vmem_limit_bytes=24 << 20),
         name="project",
-    )(low, high, late, upper, h_two, gates)
+    )(near_by(low), near_by(high), late, upper, h_two, gates)
     parts = lax.all_to_all(part, "chan", split_axis=0, concat_axis=0, tiled=True)
     gate_grad = jnp.sum(parts[:, 0], axis=0)[:slots].astype(jnp.bfloat16)
     d_input = pl.pallas_call(
@@ -337,6 +347,7 @@
         in_specs=vmem(4),
         out_specs=vmem(1)[0],
         scratch_shapes=[pltpu.VMEM((tokens, slots, hidden), jnp.bfloat16)],
+        compiler_params=pltpu.CompilerParams(vmem_limit_bytes=24 << 20),
         name="back",
     )(d_two, slope, taps, kernel)
     d_input = d_input.reshape(tokens, CAP, sections, feat).transpose(2, 1, 0, 3)

time: 166 us -> 160 us (0.964)
  blocking collectives: 43.7 us -> 69.2 us
  starting transfers between devices: 61.3 us -> 40.3 us
  Pallas kernels: 19.7 us -> 7.25 us
  waiting for transfers between devices: 32.3 us -> 35.1 us
    all_to_all x0 -> x1, blocking collectives: none -> 25.3 us  [exchange(): lax.all_to_all(array, 'expert', split_axis=0, concat_axis=0, tiled=True)]
    all_to_all x2 -> x1, starting transfers between devices: 34.3 us -> 15.8 us  [exchange(): lax.all_to_all(array, 'expert', split_axis=0, concat_axis=0, tiled=True)]
    all_to_all x2 -> x1, waiting for transfers between devices: 15.8 us -> 7.4 us  [exchange(): lax.all_to_all(array, 'expert', split_axis=0, concat_axis=0, tiled=True)]
    ppermute x4, waiting for transfers between devices: 0.29 us -> 8.37 us  [shift(): lax.ppermute(array, 'chan', [(c, (c + by) % chans) for c in range(chans)])]
    all_to_all x1, waiting for transfers between devices: 16.2 us -> 19.4 us  [on_device(): lax.all_to_all(part, 'chan', split_axis=0, concat_axis=0, tiled=True)]
    pallas_call x1, Pallas kernels: 5.35 us -> 2.19 us  [on_device(): pl.pallas_call(early_kernel, out_shape=(jax.ShapeDtypeStruct((tokens * sl...]
    pallas_call x1, Pallas kernels: 3.59 us -> 1.32 us  [on_device(): pl.pallas_call(lambda *refs: back_kernel(*refs, side=side), out_shape=jax...]
    pallas_call x1, Pallas kernels: 3.5 us -> 1.22 us  [on_device(): pl.pallas_call(lambda *refs: forward_kernel(*refs, side=side), out_shape=...]
  transfers between devices with their start and end apart: 7 -> 6, of which waited for: 4 -> 5; matrix products, arithmetic and copies ran while one was open for 1% -> 0% of each run, Pallas kernels for 8% -> 3%
where the time goes in v5:
time: 160 us; the launch traced here: 159 us
  blocking collectives  69.2 us (43%)
  starting transfers between devices  40.3 us (25%)
  waiting for transfers between devices  35.1 us (22%)
  Pallas kernels  7.25 us (5%)
  local copies, waits for them, and re-layouts  6.06 us (4%)
    all_gather x1, blocking collectives, on_device(): own = lax.all_gather(packed, 'chan', axis=0, axis_index_groups=families)  43.9 us
    all_to_all x1, blocking collectives, exchange(): lax.all_to_all(array, 'expert', split_axis=0, concat_axis=0, tiled=True)  25.3 us
    all_to_all x1, waiting for transfers between devices, on_device(): lax.all_to_all(part, 'chan', split_axis=0, concat_axis=0, tiled=True)  19.4 us
    all_to_all x1, starting transfers between devices, exchange(): lax.all_to_all(array, 'expert', split_axis=0, concat_axis=0, tiled=True)  15.8 us
    ppermute x4, starting transfers between devices, shift(): lax.ppermute(array, 'chan', [(c, (c + by) % chans) for c in range(chans)])  13.4 us
    all_to_all x1, starting transfers between devices, on_device(): lax.all_to_all(part, 'chan', split_axis=0, concat_axis=0, tiled=True)  11.1 us
    ppermute x4, waiting for transfers between devices, shift(): lax.ppermute(array, 'chan', [(c, (c + by) % chans) for c in range(chans)])  8.37 us
    all_to_all x1, waiting for transfers between devices, exchange(): lax.all_to_all(array, 'expert', split_axis=0, concat_axis=0, tiled=True)  7.4 us
  transfers between devices with their start and end apart: 6, of which 5 were waited for; matrix products, arithmetic and copies ran while one was open for 0% of the time, Pallas kernels for 3%

profile of v5, /device:TPU:1, one launch (start us, length us, event | category | flops | bytes accessed | tf_op | source)
XLA Modules:
  0.0 159.4 jit_solution(15468941794690842519)
XLA Ops:
  0.6 0.0 copy-start.3
  0.6 0.9 copy-done.3
  1.5 0.9 copy-done.4
  2.4 0.7 copy-done.8
  3.1 0.7 copy-done.9
  3.7 0.4 prep.1
  4.1 0.0 copy-start.11
  4.1 25.3 %all_to_all.15.in_ref = bf16[32,24,128]{2,1,0:T(8,128)(2,1)S(1)} all-to-all(bf16[32,24,128]{2,1,0:T(8,128)(2,1)S(1)} %prep.1), channel_id=1, replica_groups=mesh['expert'=32,'chan'=32] {'expert'}, dimensions={0} | all-to-all | bytes 393216 | tf_op jit(solution)/shard_map/all_to_all | solution.py:236
  29.4 0.2 sort.1
  29.6 0.0 copy-start.6
  29.6 43.9 %all-gather = bf16[2304,128]{1,0:T(8,128)(2,1)S(1)} all-gather(bf16[288,128]{1,0:T(8,128)(2,1)S(1)} %get-tuple-element.11), channel_id=2, replica_groups={{0,4,8,12,16,20,24,28},{1,5,9,13,17,21,25,29},{2,6,10,14,18,22,26,30},{..., dimensions={0}, use_global_device_ids=true | all-gather | bytes 663552 | tf_op jit(solution)/shard_map/all_gather | solution.py:269
  73.5 0.0 copy-done.1
  73.5 3.0 %collective-permute-start = (bf16[8,288,128]{2,1,0:T(8,128)(2,1)S(1)}, bf16[8,288,128]{2,1,0:T(8,128)(2,1)S(1)}, u32[]{:S(2)}, u32[]{:S(2)}) collective-permute-start(bf16[8,288,128]{2,1,0:T(8,128)(2,1)S(1)} %bitcast.34), channel_id=1, source_target_pairs={{0,1},{1,2},{2,3},{3,4},{4,5},{5,6},{6,7},{7,8},{8,9},{9,10},{10,1... | collective-permute-start | bytes 1769480 | tf_op jit(solution)/shard_map/ppermute | solution.py:272
  76.5 0.0 copy-done.6
  76.5 3.7 %collective-permute-start.2 = (bf16[8,288,128]{2,1,0:T(8,128)(2,1)S(1)}, bf16[8,288,128]{2,1,0:T(8,128)(2,1)S(1)}, u32[]{:S(2)}, u32[]{:S(2)}) collective-permute-start(bf16[8,288,128]{2,1,0:T(8,128)(2,1)S(1)} %bitcast.35), channel_id=1, source_target_pairs={{0,31},{1,0},{2,1},{3,2},{4,3},{5,4},{6,5},{7,6},{8,7},{9,8},{10,9... | collective-permute-start | bytes 1769480 | tf_op jit(solution)/shard_map/ppermute | solution.py:272
  80.2 5.7 %collective-permute-done.prev_ref = bf16[8,288,128]{2,1,0:T(8,128)(2,1)S(1)} collective-permute-done((bf16[8,288,128]{2,1,0:T(8,128)(2,1)S(1)}, bf16[8,288,128]{2,1,0:T(8,128)(2,1)S(1)}, u32[]{:S(2)}, u32[]{:S(2)}) %collective-permute-start) | collective-permute-done | bytes 589856 | tf_op jit(solution)/shard_map/ppermute | solution.py:272
  85.9 1.9 %collective-permute-start.1 = (bf16[4,288,128]{2,1,0:T(8,128)(2,1)S(1)}, bf16[4,288,128]{2,1,0:T(8,128)(2,1)S(1)}, u32[]{:S(2)}, u32[]{:S(2)}) collective-permute-start(bf16[4,288,128]{2,1,0:T(8,128)(2,1)S(1)} %slice.29), channel_id=1, source_target_pairs={{0,1},{1,2},{2,3},{3,4},{4,5},{5,6},{6,7},{7,8},{8,9},{9,10},{10,1... | collective-permute-start | bytes 884744 | tf_op jit(solution)/shard_map/ppermute | solution.py:272
  87.9 0.0 collective-permute-done.2.next_ref
  87.9 0.0 copy-start.2
  87.9 0.0 copy-start.5
  87.9 4.8 %collective-permute-start.3 = (bf16[4,288,128]{2,1,0:T(8,128)(2,1)S(1)}, bf16[4,288,128]{2,1,0:T(8,128)(2,1)S(1)}, u32[]{:S(2)}, u32[]{:S(2)}) collective-permute-start(bf16[4,288,128]{2,1,0:T(8,128)(2,1)S(1)} %slice.30), channel_id=1, source_target_pairs={{0,31},{1,0},{2,1},{3,2},{4,3},{5,4},{6,5},{7,6},{8,7},{9,8},{10,9... | collective-permute-start | bytes 884744 | tf_op jit(solution)/shard_map/ppermute | solution.py:272
  92.7 0.0 copy-start
  92.7 0.1 bitcast_select_fusion.1
  92.9 1.2 forward.1
  94.1 0.2 copy-done
  94.3 2.2 %early.1 = (f32[576,512]{1,0:T(8,128)S(1)}, bf16[512,512]{1,0:T(8,128)(2,1)S(1)}) custom-call(s32[1]{0:T(128)} %bitcast.10.turn_ref, bf16[8,288,128]{2,1,0:T(8,128)(2,1)S(1)} %bitcast.36, bf16[8,288,128]{2,1,0:T(8,128)(2,1)S(1)} %collective-permute-done.2.next_ref, bf16[8,288,128]{2,1,0:T(8,128)(2,1)S(1)} %collective-permute-done.prev_ref, ...), custom_call_target="tpu_custom_call" | custom-call | tf_op jit(solution)/shard_map/early/pallas_call | solution.py:302
  96.5 0.9 collective-permute-done.1.low_ref
  97.4 1.8 %collective-permute-done.3.high_ref = bf16[4,288,128]{2,1,0:T(8,128)(2,1)S(1)} collective-permute-done((bf16[4,288,128]{2,1,0:T(8,128)(2,1)S(1)}, bf16[4,288,128]{2,1,0:T(8,128)(2,1)S(1)}, u32[]{:S(2)}, u32[]{:S(2)}) %collective-permute-start.3) | collective-permute-done | bytes 294944 | tf_op jit(solution)/shard_map/ppermute | solution.py:272
  99.2 0.0 copy-done.7
  99.2 2.0 %project.1 = (bf16[9,64,512]{2,1,0:T(8,128)(2,1)S(1)}, f32[32,1,128]{2,1,0:T(1,128)}) custom-call(bf16[4,288,128]{2,1,0:T(8,128)(2,1)S(1)} %collective-permute-done.1.low_ref, bf16[4,288,128]{2,1,0:T(8,128)(2,1)S(1)} %collective-permute-done.3.high_ref, bf16[512,512]{1,0:T(8,128)(2,1)S(1)} %get-tuple-element.12.late_ref, ...), custom_call_target="tpu_custom_call" | custom-call | tf_op jit(solution)/shard_map/project/pallas_call | solution.py:316
  101.2 11.1 %all-to-all-start.1 = ((f32[32,1,128]{2,1,0:T(1,128)}), f32[32,1,128]{2,1,0:T(1,128)S(1)}, u32[]{:S(2)}, u32[]{:S(2)}) async-start(f32[32,1,128]{2,1,0:T(1,128)} %get-tuple-element.19), calls=%async_computation.1 | async-start | bytes 32768 | tf_op jit(solution)/shard_map/all_to_all | solution.py:342
  112.3 0.0 copy-done.10
  112.3 0.2 convert_reduce_fusion
  112.5 1.3 back.1
  113.8 0.1 copy.27
  113.9 0.2 reshape.46
  114.1 19.4 %all-to-all-done.1 = f32[32,1,128]{2,1,0:T(1,128)S(1)} async-done(((f32[32,1,128]{2,1,0:T(1,128)}), f32[32,1,128]{2,1,0:T(1,128)S(1)}, u32[]{:S(2)}, u32[]{:S(2)}) %all-to-all-start.1) | async-done | bytes 16416 | tf_op jit(solution)/shard_map/all_to_all | solution.py:342
  133.5 0.1 reduce_sum.22
  133.5 0.1 convert_element_type.15
  133.6 0.1 copy.23
  133.7 0.1 fusion.1
  133.8 0.7 copy.24
  134.5 15.8 %all-to-all-start.2 = ((bf16[32,2,640]{2,1,0:T(2,128)(2,1)}), bf16[32,2,640]{2,1,0:T(2,128)(2,1)S(1)}, u32[]{:S(2)}, u32[]{:S(2)}) async-start(bf16[32,2,640]{2,1,0:T(2,128)(2,1)} %copy.24), calls=%async_computation.2 | async-start | bytes 163840 | tf_op jit(solution)/shard_map/all_to_all | solution.py:236
  150.3 7.4 %all-to-all-done.2 = bf16[32,2,640]{2,1,0:T(2,128)(2,1)S(1)} async-done(((bf16[32,2,640]{2,1,0:T(2,128)(2,1)}), bf16[32,2,640]{2,1,0:T(2,128)(2,1)S(1)}, u32[]{:S(2)}, u32[]{:S(2)}) %all-to-all-start.2) | async-done | bytes 81952 | tf_op jit(solution)/shard_map/all_to_all | solution.py:236
  157.8 0.2 convolution_convert_fusion
  157.9 0.7 slice_reduce_fusion
  158.7 0.1 reshape.48
  158.8 0.6 copy.25
  (15 shorter events, 0.1 us)
Async XLA Ops:
  0.6 0.9 copy-start.3
  1.5 0.9 copy-start.4
  2.4 0.7 copy-start.8
  3.1 0.7 copy-start.9
  4.1 88.6 %copy-start.11 = (bf16[1,3,3,32,512]{4,3,2,1,0:T(8,128)(2,1)S(1)}, bf16[1,3,3,32,512]{4,3,2,1,0:T(8,128)(2,1)}, u32[]{:S(2)}) copy-start(bf16[1,3,3,32,512]{4,3,2,1,0:T(8,128)(2,1)} %param.11) | copy-start | bytes 884740
  29.6 43.9 %copy-start.1 = (bf16[9,64,64]{2,1,0:T(8,128)(2,1)}, bf16[9,64,64]{2,1,0:T(8,128)(2,1)S(1)}, u32[]{:S(2)}) copy-start(bf16[9,64,64]{2,1,0:T(8,128)(2,1)S(1)} %get-tuple-element.14.refs_0_) | copy-start | bytes 221188
  29.6 46.9 %copy-start.6 = (f32[64,128]{1,0:T(8,128)}, f32[64,128]{1,0:T(8,128)S(1)}, u32[]{:S(2)}) copy-start(f32[64,128]{1,0:T(8,128)S(1)} %get-tuple-element.16.gate_ref) | copy-start | bytes 98308
  73.5 12.4 %collective-permute-start = (bf16[8,288,128]{2,1,0:T(8,128)(2,1)S(1)}, bf16[8,288,128]{2,1,0:T(8,128)(2,1)S(1)}, u32[]{:S(2)}, u32[]{:S(2)}) collective-permute-start(bf16[8,288,128]{2,1,0:T(8,128)(2,1)S(1)} %bitcast.34), channel_id=1, source_target_pairs={{0,1},{1,2},{2,3},{3,4},{4,5},{5,6},{6,7},{7,8},{8,9},{9,10},{10,1... | collective-permute-start | bytes 1769480 | tf_op jit(solution)/shard_map/ppermute | solution.py:272
  76.5 11.4 %collective-permute-start.2 = (bf16[8,288,128]{2,1,0:T(8,128)(2,1)S(1)}, bf16[8,288,128]{2,1,0:T(8,128)(2,1)S(1)}, u32[]{:S(2)}, u32[]{:S(2)}) collective-permute-start(bf16[8,288,128]{2,1,0:T(8,128)(2,1)S(1)} %bitcast.35), channel_id=1, source_target_pairs={{0,31},{1,0},{2,1},{3,2},{4,3},{5,4},{6,5},{7,6},{8,7},{9,8},{10,9... | collective-permute-start | bytes 1769480 | tf_op jit(solution)/shard_map/ppermute | solution.py:272
  85.9 11.5 %collective-permute-start.1 = (bf16[4,288,128]{2,1,0:T(8,128)(2,1)S(1)}, bf16[4,288,128]{2,1,0:T(8,128)(2,1)S(1)}, u32[]{:S(2)}, u32[]{:S(2)}) collective-permute-start(bf16[4,288,128]{2,1,0:T(8,128)(2,1)S(1)} %slice.29), channel_id=1, source_target_pairs={{0,1},{1,2},{2,3},{3,4},{4,5},{5,6},{6,7},{7,8},{8,9},{9,10},{10,1... | collective-permute-start | bytes 884744 | tf_op jit(solution)/shard_map/ppermute | solution.py:272
  87.9 4.9 %copy-start.2 = (bf16[9,64,64]{2,1,0:T(8,128)(2,1)S(1)}, bf16[9,64,64]{2,1,0:T(8,128)(2,1)}, u32[]{:S(2)}) copy-start(bf16[9,64,64]{2,1,0:T(8,128)(2,1)} %copy-done.1) | copy-start | bytes 221188
  87.9 4.9 %copy-start.5 = (bf16[1,9,512]{2,1,0:T(8,128)(2,1)S(1)}, bf16[1,9,512]{2,1,0:T(8,128)(2,1)}, u32[]{:S(2)}) copy-start(bf16[1,9,512]{2,1,0:T(8,128)(2,1)} %param.12) | copy-start | bytes 27652
  87.9 11.3 %collective-permute-start.3 = (bf16[4,288,128]{2,1,0:T(8,128)(2,1)S(1)}, bf16[4,288,128]{2,1,0:T(8,128)(2,1)S(1)}, u32[]{:S(2)}, u32[]{:S(2)}) collective-permute-start(bf16[4,288,128]{2,1,0:T(8,128)(2,1)S(1)} %slice.30), channel_id=1, source_target_pairs={{0,31},{1,0},{2,1},{3,2},{4,3},{5,4},{6,5},{7,6},{8,7},{9,8},{10,9... | collective-permute-start | bytes 884744 | tf_op jit(solution)/shard_map/ppermute | solution.py:272
  92.7 1.6 %copy-start = (bf16[1,512,2048]{2,1,0:T(8,128)(2,1)S(1)}, bf16[1,512,2048]{2,1,0:T(8,128)(2,1)}, u32[]{:S(2)}) copy-start(bf16[1,512,2048]{2,1,0:T(8,128)(2,1)} %param.13) | copy-start | bytes 6291460
  94.3 4.9 %copy-start.7 = (f32[64,128]{1,0:T(8,128)S(1)}, f32[64,128]{1,0:T(8,128)}, u32[]{:S(2)}) copy-start(f32[64,128]{1,0:T(8,128)} %copy-done.6) | copy-start | bytes 98308
  99.2 13.1 %copy-start.10 = (s32[32,1]{0,1:T(1,128)S(1)}, s32[32,1]{0,1:T(1,128)}, u32[]{:S(2)}) copy-start(s32[32,1]{0,1:T(1,128)} %param.10) | copy-start | bytes 388
  101.2 32.3 %all-to-all-start.1 = ((f32[32,1,128]{2,1,0:T(1,128)}), f32[32,1,128]{2,1,0:T(1,128)S(1)}, u32[]{:S(2)}, u32[]{:S(2)}) async-start(f32[32,1,128]{2,1,0:T(1,128)} %get-tuple-element.19), calls=%async_computation.1 | async-start | bytes 32768 | tf_op jit(solution)/shard_map/all_to_all | solution.py:342
  134.5 23.2 %all-to-all-start.2 = ((bf16[32,2,640]{2,1,0:T(2,128)(2,1)}), bf16[32,2,640]{2,1,0:T(2,128)(2,1)S(1)}, u32[]{:S(2)}, u32[]{:S(2)}) async-start(bf16[32,2,640]{2,1,0:T(2,128)(2,1)} %copy.24), calls=%async_computation.2 | async-start | bytes 163840 | tf_op jit(solution)/shard_map/all_to_all | solution.py:236

commit v6 on v5

--- a/solution.py
+++ b/solution.py
@@ -91,8 +91,19 @@
             h_two_ref[pos, :, span] = total.astype(jnp.bfloat16)
 
 
-def early_kernel(turn_ref, own_ref, next_ref, prev_ref, weight_ref, upper_ref, late_ref, left_ref):
-    steps, rows, lanes = own_ref.shape
+def split_kernel(in_ref, low_ref, high_ref):
+    steps = low_ref.shape[0]
+    low_ref[...] = in_ref[:steps]
+    high_ref[...] = in_ref[steps:]
+
+
+def early_kernel(
+    turn_ref, own_low, own_high, next_low, next_high, prev_low, prev_high, weight_ref,
+    upper_ref, late_ref, left_ref,
+):
+    part_steps, rows, lanes = own_low.shape
+    steps = 2 * part_steps
+    families = ((own_low, own_high), (next_low, next_high), None, (prev_low, prev_high))
     half = lanes // 2
     hidden = weight_ref.shape[0]
     blank = jnp.zeros((rows, half), jnp.bfloat16)
@@ -104,8 +115,11 @@
             for step in range(steps):
                 for pair in range(2):
                     kinds = [(2 * pair + side - turn) % 4 for side in range(2)]
-                    refs = [(own_ref, next_ref, None, prev_ref)[kind] for kind in kinds]
-                    blocks = [None if ref is None else ref[step] for ref in refs]
+                    refs = [families[kind] for kind in kinds]
+                    blocks = [
+                        None if ref is None else ref[step // part_steps][step % part_steps]
+                        for ref in refs
+                    ]
                     start = (2 * step + pair) * lanes
                     for group in range(2):
                         part = slice(group * half, (group + 1) * half)
@@ -242,7 +256,6 @@
         out_shape=jax.ShapeDtypeStruct((sections, lines, CAP * feat), jnp.bfloat16),
         in_specs=vmem(4),
         out_specs=vmem(1)[0],
-        compiler_params=pltpu.CompilerParams(vmem_limit_bytes=24 << 20),
         name="prep",
     )(
         expert_id.reshape(1, owned),
@@ -271,10 +284,21 @@
     def shift(array, by):
         return lax.ppermute(array, "chan", [(c, (c + by) % chans) for c in range(chans)])
 
-    prev = shift(own, 1)
-    following = shift(own, -1)
-    low = shift(prev[: steps // 2], 1)
-    high = shift(following[steps // 2 :], -1)
+    part = jax.ShapeDtypeStruct((steps // 2, *own.shape[1:]), own.dtype)
+    own_low, own_high = pl.pallas_call(
+        split_kernel,
+        out_shape=(part, part),
+        in_specs=vmem(1),
+        out_specs=tuple(vmem(2)),
+        compiler_params=pltpu.CompilerParams(vmem_limit_bytes=24 << 20),
+        name="split",
+    )(near_by(own))
+    prev_low = shift(own_low, 1)
+    next_high = shift(own_high, -1)
+    prev_high = shift(own_high, 1)
+    next_low = shift(own_low, -1)
+    low = shift(prev_low, 1)
+    high = shift(next_high, -1)
     turn = (lax.axis_index("chan") % 4).astype(jnp.int32).reshape(1)
 
     taps = w_depth[0]
@@ -305,12 +329,16 @@
             jax.ShapeDtypeStruct((tokens * slots, hidden), jnp.float32),
             jax.ShapeDtypeStruct((hidden, features // 4), jnp.bfloat16),
         ),
-        in_specs=[pl.BlockSpec(memory_space=pltpu.SMEM)] + vmem(4),
+        in_specs=[pl.BlockSpec(memory_space=pltpu.SMEM)] + vmem(7),
         out_specs=tuple(vmem(2)),
         scratch_shapes=[pltpu.VMEM((tokens * slots, features), jnp.bfloat16)],
         compiler_params=pltpu.CompilerParams(vmem_limit_bytes=24 << 20),
         name="early",
-    )(turn, near_by(own), near_by(following), near_by(prev), near_by(w_out[0]))
+    )(
+        turn,
+        *[near_by(x) for x in (own_low, own_high, next_low, next_high, prev_low, prev_high)],
+        near_by(w_out[0]),
+    )
     wide = 256
     whole = lambda shape: pl.BlockSpec(shape, lambda i: (0,) * len(shape))
     d_two, part = pl.pallas_call(

time: 160 us -> 154 us (0.963)
  waiting for transfers between devices: 35.1 us -> 29.3 us
  local copies, waits for them, and re-layouts: 6.06 us -> 2.91 us
  starting transfers between devices: 40.3 us -> 42.6 us
  Pallas kernels: 7.25 us -> 8.97 us
    ppermute x4 -> x6, waiting for transfers between devices: 8.37 us -> 2.55 us  [shift(): lax.ppermute(array, 'chan', [(c, (c + by) % chans) for c in range(chans)])]
    ppermute x4 -> x6, starting transfers between devices: 13.4 us -> 18.9 us  [shift(): lax.ppermute(array, 'chan', [(c, (c + by) % chans) for c in range(chans)])]
    all_to_all x1, starting transfers between devices: 15.8 us -> 11.8 us  [exchange(): lax.all_to_all(array, 'expert', split_axis=0, concat_axis=0, tiled=True)]
    unnamed x25 -> x9, local copies, waits for them, and re-layouts: 3.96 us -> 0.86 us
    pallas_call x1, Pallas kernels: 0.42 us -> 2.09 us  [on_device(): pl.pallas_call(prep_kernel, out_shape=jax.ShapeDtypeStruct((sections, lin...]
  transfers between devices with their start and end apart: 6 -> 8, of which waited for: 5 -> 4; matrix products, arithmetic and copies ran while one was open for 0% -> 0% of each run, Pallas kernels for 3% -> 3%
where the time goes in v6:
time: 154 us
  blocking collectives  68.5 us (44%)
  starting transfers between devices  42.6 us (28%)
  waiting for transfers between devices  29.3 us (19%)
  Pallas kernels  8.97 us (6%)
  local copies, waits for them, and re-layouts  2.91 us (2%)
    all_gather x1, blocking collectives, on_device(): own = lax.all_gather(packed, 'chan', axis=0, axis_index_groups=families)  42.5 us
    all_to_all x1, blocking collectives, exchange(): lax.all_to_all(array, 'expert', split_axis=0, concat_axis=0, tiled=True)  26 us
    all_to_all x1, waiting for transfers between devices, on_device(): lax.all_to_all(part, 'chan', split_axis=0, concat_axis=0, tiled=True)  19.4 us
    ppermute x6, starting transfers between devices, shift(): lax.ppermute(array, 'chan', [(c, (c + by) % chans) for c in range(chans)])  18.9 us
    all_to_all x1, starting transfers between devices, on_device(): lax.all_to_all(part, 'chan', split_axis=0, concat_axis=0, tiled=True)  11.9 us
    all_to_all x1, starting transfers between devices, exchange(): lax.all_to_all(array, 'expert', split_axis=0, concat_axis=0, tiled=True)  11.8 us
    all_to_all x1, waiting for transfers between devices, exchange(): lax.all_to_all(array, 'expert', split_axis=0, concat_axis=0, tiled=True)  7.41 us
  transfers between devices with their start and end apart: 8, of which 4 were waited for; matrix products, arithmetic and copies ran while one was open for 0% of the time, Pallas kernels for 3%

profile of v6, /device:TPU:1, one launch (start us, length us, event | category | flops | bytes accessed | tf_op | source)
XLA Modules:
  0.0 153.7 jit_solution(5799484019335731195)
XLA Ops:
  0.6 0.0 copy-start.2
  0.6 2.1 %prep.1 = bf16[32,24,128]{2,1,0:T(8,128)(2,1)} custom-call(s32[1,32]{1,0:T(1,128)} %bitcast.44, bf16[1,32]{1,0:T(2,128)(2,1)} %bitcast.43, bf16[9,32,64]{2,1,0:T(8,128)(2,1)} %bitcast.41, bf16[9,32,64]{2,1,0:T(8,128)(2,1)} %bitcast.42), custom_call_target="tpu_custom_call" | custom-call | tf_op jit(solution)/shard_map/prep/pallas_call | solution.py:254
  2.7 26.0 %all_to_all.15.in_ref = bf16[32,24,128]{2,1,0:T(8,128)(2,1)S(1)} all-to-all(bf16[32,24,128]{2,1,0:T(8,128)(2,1)} %prep.1), channel_id=1, replica_groups=mesh['expert'=32,'chan'=32] {'expert'}, dimensions={0} | all-to-all | bytes 393216 | tf_op jit(solution)/shard_map/all_to_all | solution.py:250
  28.8 0.2 sort.1
  28.9 42.5 %all-gather = bf16[2304,128]{1,0:T(8,128)(2,1)S(1)} all-gather(bf16[288,128]{1,0:T(8,128)(2,1)S(1)} %get-tuple-element.13), channel_id=2, replica_groups={{0,4,8,12,16,20,24,28},{1,5,9,13,17,21,25,29},{2,6,10,14,18,22,26,30},{..., dimensions={0}, use_global_device_ids=true | all-gather | bytes 663552 | tf_op jit(solution)/shard_map/all_gather | solution.py:282
  71.4 0.0 copy-start.1
  71.4 2.4 %collective-permute-start = (bf16[4,288,128]{2,1,0:T(8,128)(2,1)S(1)}, bf16[4,288,128]{2,1,0:T(8,128)(2,1)S(1)}, u32[]{:S(2)}, u32[]{:S(2)}) collective-permute-start(bf16[4,288,128]{2,1,0:T(8,128)(2,1)S(1)} %get-tuple-element.14.own_low), channel_id=1, source_target_pairs={{0,1},{1,2},{2,3},{3,4},{4,5},{5,6},{6,7},{7,8},{8,9},{9,10},{10,1... | collective-permute-start | bytes 884744 | tf_op jit(solution)/shard_map/ppermute | solution.py:285
  73.8 4.7 %collective-permute-start.2 = (bf16[4,288,128]{2,1,0:T(8,128)(2,1)S(1)}, bf16[4,288,128]{2,1,0:T(8,128)(2,1)S(1)}, u32[]{:S(2)}, u32[]{:S(2)}) collective-permute-start(bf16[4,288,128]{2,1,0:T(8,128)(2,1)S(1)} %get-tuple-element.15.own_high), channel_id=1, source_target_pairs={{0,31},{1,0},{2,1},{3,2},{4,3},{5,4},{6,5},{7,6},{8,7},{9,8},{10,9... | collective-permute-start | bytes 884744 | tf_op jit(solution)/shard_map/ppermute | solution.py:285
  78.6 3.4 %collective-permute-start.4 = (bf16[4,288,128]{2,1,0:T(8,128)(2,1)S(1)}, bf16[4,288,128]{2,1,0:T(8,128)(2,1)S(1)}, u32[]{:S(2)}, u32[]{:S(2)}) collective-permute-start(bf16[4,288,128]{2,1,0:T(8,128)(2,1)S(1)} %get-tuple-element.14.own_low), channel_id=1, source_target_pairs={{0,31},{1,0},{2,1},{3,2},{4,3},{5,4},{6,5},{7,6},{8,7},{9,8},{10,9... | collective-permute-start | bytes 884744 | tf_op jit(solution)/shard_map/ppermute | solution.py:285
  81.9 1.9 %collective-permute-start.5 = (bf16[4,288,128]{2,1,0:T(8,128)(2,1)S(1)}, bf16[4,288,128]{2,1,0:T(8,128)(2,1)S(1)}, u32[]{:S(2)}, u32[]{:S(2)}) collective-permute-start(bf16[4,288,128]{2,1,0:T(8,128)(2,1)S(1)} %get-tuple-element.15.own_high), channel_id=1, source_target_pairs={{0,1},{1,2},{2,3},{3,4},{4,5},{5,6},{6,7},{7,8},{8,9},{9,10},{10,1... | collective-permute-start | bytes 884744 | tf_op jit(solution)/shard_map/ppermute | solution.py:285
  83.9 0.0 collective-permute-done.prev_low
  83.9 1.9 %collective-permute-start.1 = (bf16[4,288,128]{2,1,0:T(8,128)(2,1)S(1)}, bf16[4,288,128]{2,1,0:T(8,128)(2,1)S(1)}, u32[]{:S(2)}, u32[]{:S(2)}) collective-permute-start(bf16[4,288,128]{2,1,0:T(8,128)(2,1)S(1)} %collective-permute-done.prev_low), channel_id=1, source_target_pairs={{0,1},{1,2},{2,3},{3,4},{4,5},{5,6},{6,7},{7,8},{8,9},{9,10},{10,1... | collective-permute-start | bytes 884744 | tf_op jit(solution)/shard_map/ppermute | solution.py:285
  85.8 0.0 collective-permute-done.2.next_high
  85.8 4.6 %collective-permute-start.3 = (bf16[4,288,128]{2,1,0:T(8,128)(2,1)S(1)}, bf16[4,288,128]{2,1,0:T(8,128)(2,1)S(1)}, u32[]{:S(2)}, u32[]{:S(2)}) collective-permute-start(bf16[4,288,128]{2,1,0:T(8,128)(2,1)S(1)} %collective-permute-done.2.next_high), channel_id=1, source_target_pairs={{0,31},{1,0},{2,1},{3,2},{4,3},{5,4},{6,5},{7,6},{8,7},{9,8},{10,9... | collective-permute-start | bytes 884744 | tf_op jit(solution)/shard_map/ppermute | solution.py:285
  90.4 0.0 copy-done.2
  90.4 0.0 copy-start
  90.4 0.1 bitcast_select_fusion.1
  90.5 0.0 copy-done.1
  90.5 1.2 forward.1
  91.8 0.0 collective-permute-done.4.next_low
  91.8 0.0 collective-permute-done.5.prev_high
  91.8 0.2 copy-done
  92.0 2.2 %early.1 = (f32[576,512]{1,0:T(8,128)S(1)}, bf16[512,512]{1,0:T(8,128)(2,1)S(1)}) custom-call(s32[1]{0:T(128)} %bitcast.10.turn_ref, bf16[4,288,128]{2,1,0:T(8,128)(2,1)S(1)} %get-tuple-element.14.own_low, bf16[4,288,128]{2,1,0:T(8,128)(2,1)S(1)} %get-tuple-element.15.own_high, bf16[4,288,128]{2,1,0:T(8,128)(2,1)S(1)} %collective-permute-done.4.next_low, ...), custom_call_target="tpu_custom_call" | custom-call | tf_op jit(solution)/shard_map/early/pallas_call | solution.py:326
  94.2 0.7 collective-permute-done.1.low_ref
  94.9 1.8 %collective-permute-done.3.high_ref = bf16[4,288,128]{2,1,0:T(8,128)(2,1)S(1)} collective-permute-done((bf16[4,288,128]{2,1,0:T(8,128)(2,1)S(1)}, bf16[4,288,128]{2,1,0:T(8,128)(2,1)S(1)}, u32[]{:S(2)}, u32[]{:S(2)}) %collective-permute-start.3) | collective-permute-done | bytes 294944 | tf_op jit(solution)/shard_map/ppermute | solution.py:285
  96.7 0.0 copy-start.3
  96.7 2.0 %project.1 = (bf16[9,64,512]{2,1,0:T(8,128)(2,1)S(1)}, f32[32,1,128]{2,1,0:T(1,128)}) custom-call(bf16[4,288,128]{2,1,0:T(8,128)(2,1)S(1)} %collective-permute-done.1.low_ref, bf16[4,288,128]{2,1,0:T(8,128)(2,1)S(1)} %collective-permute-done.3.high_ref, bf16[512,512]{1,0:T(8,128)(2,1)S(1)} %get-tuple-element.16.late_ref, ...), custom_call_target="tpu_custom_call" | custom-call | tf_op jit(solution)/shard_map/project/pallas_call | solution.py:344
  98.7 11.9 %all-to-all-start.1 = ((f32[32,1,128]{2,1,0:T(1,128)}), f32[32,1,128]{2,1,0:T(1,128)S(1)}, u32[]{:S(2)}, u32[]{:S(2)}) async-start(f32[32,1,128]{2,1,0:T(1,128)} %get-tuple-element.23), calls=%async_computation.1 | async-start | bytes 32768 | tf_op jit(solution)/shard_map/all_to_all | solution.py:370
  110.6 0.0 copy-done.3
  110.6 0.2 convert_reduce_fusion
  110.8 1.3 back.1
  112.1 0.1 copy.27
  112.3 0.2 reshape.46
  112.5 19.4 %all-to-all-done.1 = f32[32,1,128]{2,1,0:T(1,128)S(1)} async-done(((f32[32,1,128]{2,1,0:T(1,128)}), f32[32,1,128]{2,1,0:T(1,128)S(1)}, u32[]{:S(2)}, u32[]{:S(2)}) %all-to-all-start.1) | async-done | bytes 16416 | tf_op jit(solution)/shard_map/all_to_all | solution.py:370
  131.8 0.1 reduce_sum.22
  131.9 0.1 convert_element_type.15
  131.9 0.1 copy.23
  132.1 0.1 fusion.1
  132.1 0.7 copy.24
  132.8 11.8 %all-to-all-start.2 = ((bf16[32,2,640]{2,1,0:T(2,128)(2,1)}), bf16[32,2,640]{2,1,0:T(2,128)(2,1)S(1)}, u32[]{:S(2)}, u32[]{:S(2)}) async-start(bf16[32,2,640]{2,1,0:T(2,128)(2,1)} %copy.24), calls=%async_computation.2 | async-start | bytes 163840 | tf_op jit(solution)/shard_map/all_to_all | solution.py:250
  144.6 7.4 %all-to-all-done.2 = bf16[32,2,640]{2,1,0:T(2,128)(2,1)S(1)} async-done(((bf16[32,2,640]{2,1,0:T(2,128)(2,1)}), bf16[32,2,640]{2,1,0:T(2,128)(2,1)S(1)}, u32[]{:S(2)}, u32[]{:S(2)}) %all-to-all-start.2) | async-done | bytes 81952 | tf_op jit(solution)/shard_map/all_to_all | solution.py:250
  152.1 0.2 convolution_convert_fusion
  152.3 0.7 slice_reduce_fusion
  153.0 0.1 reshape.48
  153.1 0.6 copy.25
  (5 shorter events, 0.1 us)
Async XLA Ops:
  0.6 89.8 %copy-start.2 = (bf16[1,3,3,32,512]{4,3,2,1,0:T(8,128)(2,1)S(1)}, bf16[1,3,3,32,512]{4,3,2,1,0:T(8,128)(2,1)}, u32[]{:S(2)}) copy-start(bf16[1,3,3,32,512]{4,3,2,1,0:T(8,128)(2,1)} %param.11) | copy-start | bytes 884740
  71.4 19.1 %copy-start.1 = (bf16[1,9,512]{2,1,0:T(8,128)(2,1)S(1)}, bf16[1,9,512]{2,1,0:T(8,128)(2,1)}, u32[]{:S(2)}) copy-start(bf16[1,9,512]{2,1,0:T(8,128)(2,1)} %param.12) | copy-start | bytes 27652
  71.4 12.4 %collective-permute-start = (bf16[4,288,128]{2,1,0:T(8,128)(2,1)S(1)}, bf16[4,288,128]{2,1,0:T(8,128)(2,1)S(1)}, u32[]{:S(2)}, u32[]{:S(2)}) collective-permute-start(bf16[4,288,128]{2,1,0:T(8,128)(2,1)S(1)} %get-tuple-element.14.own_low), channel_id=1, source_target_pairs={{0,1},{1,2},{2,3},{3,4},{4,5},{5,6},{6,7},{7,8},{8,9},{9,10},{10,1... | collective-permute-start | bytes 884744 | tf_op jit(solution)/shard_map/ppermute | solution.py:285
  73.8 12.0 %collective-permute-start.2 = (bf16[4,288,128]{2,1,0:T(8,128)(2,1)S(1)}, bf16[4,288,128]{2,1,0:T(8,128)(2,1)S(1)}, u32[]{:S(2)}, u32[]{:S(2)}) collective-permute-start(bf16[4,288,128]{2,1,0:T(8,128)(2,1)S(1)} %get-tuple-element.15.own_high), channel_id=1, source_target_pairs={{0,31},{1,0},{2,1},{3,2},{4,3},{5,4},{6,5},{7,6},{8,7},{9,8},{10,9... | collective-permute-start | bytes 884744 | tf_op jit(solution)/shard_map/ppermute | solution.py:285
  78.6 13.2 %collective-permute-start.4 = (bf16[4,288,128]{2,1,0:T(8,128)(2,1)S(1)}, bf16[4,288,128]{2,1,0:T(8,128)(2,1)S(1)}, u32[]{:S(2)}, u32[]{:S(2)}) collective-permute-start(bf16[4,288,128]{2,1,0:T(8,128)(2,1)S(1)} %get-tuple-element.14.own_low), channel_id=1, source_target_pairs={{0,31},{1,0},{2,1},{3,2},{4,3},{5,4},{6,5},{7,6},{8,7},{9,8},{10,9... | collective-permute-start | bytes 884744 | tf_op jit(solution)/shard_map/ppermute | solution.py:285
  81.9 9.9 %collective-permute-start.5 = (bf16[4,288,128]{2,1,0:T(8,128)(2,1)S(1)}, bf16[4,288,128]{2,1,0:T(8,128)(2,1)S(1)}, u32[]{:S(2)}, u32[]{:S(2)}) collective-permute-start(bf16[4,288,128]{2,1,0:T(8,128)(2,1)S(1)} %get-tuple-element.15.own_high), channel_id=1, source_target_pairs={{0,1},{1,2},{2,3},{3,4},{4,5},{5,6},{6,7},{7,8},{8,9},{9,10},{10,1... | collective-permute-start | bytes 884744 | tf_op jit(solution)/shard_map/ppermute | solution.py:285
  83.9 11.0 %collective-permute-start.1 = (bf16[4,288,128]{2,1,0:T(8,128)(2,1)S(1)}, bf16[4,288,128]{2,1,0:T(8,128)(2,1)S(1)}, u32[]{:S(2)}, u32[]{:S(2)}) collective-permute-start(bf16[4,288,128]{2,1,0:T(8,128)(2,1)S(1)} %collective-permute-done.prev_low), channel_id=1, source_target_pairs={{0,1},{1,2},{2,3},{3,4},{4,5},{5,6},{6,7},{7,8},{8,9},{9,10},{10,1... | collective-permute-start | bytes 884744 | tf_op jit(solution)/shard_map/ppermute | solution.py:285
  85.8 10.9 %collective-permute-start.3 = (bf16[4,288,128]{2,1,0:T(8,128)(2,1)S(1)}, bf16[4,288,128]{2,1,0:T(8,128)(2,1)S(1)}, u32[]{:S(2)}, u32[]{:S(2)}) collective-permute-start(bf16[4,288,128]{2,1,0:T(8,128)(2,1)S(1)} %collective-permute-done.2.next_high), channel_id=1, source_target_pairs={{0,31},{1,0},{2,1},{3,2},{4,3},{5,4},{6,5},{7,6},{8,7},{9,8},{10,9... | collective-permute-start | bytes 884744 | tf_op jit(solution)/shard_map/ppermute | solution.py:285
  90.4 1.6 %copy-start = (bf16[1,512,2048]{2,1,0:T(8,128)(2,1)S(1)}, bf16[1,512,2048]{2,1,0:T(8,128)(2,1)}, u32[]{:S(2)}) copy-start(bf16[1,512,2048]{2,1,0:T(8,128)(2,1)} %param.13) | copy-start | bytes 6291460
  96.7 13.9 %copy-start.3 = (s32[32,1]{0,1:T(1,128)S(1)}, s32[32,1]{0,1:T(1,128)}, u32[]{:S(2)}) copy-start(s32[32,1]{0,1:T(1,128)} %param.10) | copy-start | bytes 388
  98.7 33.1 %all-to-all-start.1 = ((f32[32,1,128]{2,1,0:T(1,128)}), f32[32,1,128]{2,1,0:T(1,128)S(1)}, u32[]{:S(2)}, u32[]{:S(2)}) async-start(f32[32,1,128]{2,1,0:T(1,128)} %get-tuple-element.23), calls=%async_computation.1 | async-start | bytes 32768 | tf_op jit(solution)/shard_map/all_to_all | solution.py:370
  132.8 19.2 %all-to-all-start.2 = ((bf16[32,2,640]{2,1,0:T(2,128)(2,1)}), bf16[32,2,640]{2,1,0:T(2,128)(2,1)S(1)}, u32[]{:S(2)}, u32[]{:S(2)}) async-start(bf16[32,2,640]{2,1,0:T(2,128)(2,1)} %copy.24), calls=%async_computation.2 | async-start | bytes 163840 | tf_op jit(solution)/shard_map/all_to_all | solution.py:250

commit v7 on v6

--- a/solution.py
+++ b/solution.py
@@ -222,6 +222,52 @@
         d_in_ref[pos] = total.astype(jnp.bfloat16)
 
 
+def merge_kernel(parts_ref, d_in_ref, out_ref):
+    tokens, slots, feat = d_in_ref.shape
+    own = slots // 2
+    totals = jnp.broadcast_to(jnp.sum(parts_ref[...], axis=0), (own, parts_ref.shape[2]))
+    rows = lax.broadcasted_iota(jnp.int32, totals.shape, 0)
+    cols = lax.broadcasted_iota(jnp.int32, totals.shape, 1)
+    lines = []
+    for pos in range(tokens):
+        field = d_in_ref[pos].astype(jnp.float32)
+        lines.append(jnp.concatenate([field[:own], field[own:]], axis=1))
+    halves = []
+    for group in range(2):
+        mine = jnp.where(cols == rows + group * own, totals, 0.0)
+        halves.append(jnp.broadcast_to(jnp.sum(mine, axis=1, keepdims=True), (own, feat)))
+    lines.append(jnp.concatenate(halves, axis=1))
+    while len(lines) < out_ref.shape[1]:
+        lines.append(jnp.zeros_like(lines[0]))
+    out_ref[...] = jnp.swapaxes(jnp.stack(lines), 0, 1).astype(jnp.bfloat16)
+
+
+def finish_kernel(ids_ref, back_ref, grads_ref, gate_ref):
+    tokens, owned, feat = grads_ref.shape
+    sections = back_ref.shape[0]
+    rows = lax.broadcasted_iota(jnp.int32, (owned, owned), 0)
+    cols = lax.broadcasted_iota(jnp.int32, (owned, owned), 1)
+    wide = jnp.broadcast_to(ids_ref[...], (owned, owned))
+    column = jnp.sum(jnp.where(rows == cols, wide, 0), axis=1, keepdims=True)
+    earlier = jnp.where((cols < rows) & (column == wide), 1, 0)
+    rank = jnp.sum(earlier, axis=1, keepdims=True)
+    named = column == lax.broadcasted_iota(jnp.int32, (owned, sections), 1)
+    picks = [jnp.where(named & (rank == r), 1.0, 0.0).astype(jnp.bfloat16) for r in range(CAP)]
+    lines = jnp.swapaxes(back_ref[...].astype(jnp.float32), 0, 1)
+
+    def pick(line):
+        line = line.astype(jnp.bfloat16)
+        return jnp.dot(
+            picks[0], line[:, :feat], preferred_element_type=jnp.float32
+        ) + jnp.dot(picks[1], line[:, feat:], preferred_element_type=jnp.float32)
+
+    for pos in range(tokens):
+        grads_ref[pos] = pick(lines[pos]).astype(jnp.bfloat16)
+    sums = jnp.broadcast_to(pick(lines[tokens])[:, :1], (owned, owned))
+    sums = jnp.sum(jnp.where(rows == cols, sums, 0.0), axis=0, keepdims=True)
+    gate_ref[...] = sums.astype(jnp.bfloat16)
+
+
 def near_by(array):
     return pltpu.with_memory_space_constraint(array, pltpu.VMEM)
 
@@ -233,23 +279,14 @@
 def on_device(tiles_in, grad_out, gate, expert_id, w_conv, w_depth, w_out):
     owned, side, _, feat = tiles_in.shape
     tokens = side * side
-    width = tokens * feat
     sections = lax.axis_size("expert")
     slots = sections * CAP
     hidden = w_out.shape[1]
     group = w_conv.shape[3]
-    chosen = expert_id[:, 0]
-    matches = (chosen[:, None] == jnp.arange(sections, dtype=jnp.int32)[None, :]).astype(jnp.int32)
-    rows = jnp.arange(owned, dtype=jnp.int32)
-    earlier = (rows[:, None] > rows[None, :]) & (chosen[:, None] == chosen[None, :])
-    rank = jnp.sum(earlier.astype(jnp.int32), axis=1)
-    slot = chosen * CAP + rank
-    placing = (slot[:, None] == jnp.arange(slots, dtype=jnp.int32)[None, :]).astype(jnp.bfloat16)
 
     def exchange(array):
         return lax.all_to_all(array, "expert", split_axis=0, concat_axis=0, tiled=True)
 
-    tail = 64
     lines = -(-(2 * tokens + 1) // 8) * 8
     outward = pl.pallas_call(
         prep_kernel,
@@ -368,7 +405,6 @@
         name="project",
     )(near_by(low), near_by(high), late, upper, h_two, gates)
     parts = lax.all_to_all(part, "chan", split_axis=0, concat_axis=0, tiled=True)
-    gate_grad = jnp.sum(parts[:, 0], axis=0)[:slots].astype(jnp.bfloat16)
     d_input = pl.pallas_call(
         lambda *refs: back_kernel(*refs, side=side),
         out_shape=jax.ShapeDtypeStruct((tokens, slots, feat), jnp.bfloat16),
@@ -378,14 +414,30 @@
         compiler_params=pltpu.CompilerParams(vmem_limit_bytes=24 << 20),
         name="back",
     )(d_two, slope, taps, kernel)
-    d_input = d_input.reshape(tokens, CAP, sections, feat).transpose(2, 1, 0, 3)
-    d_input = d_input.reshape(sections, CAP, width)
-    extra = jnp.pad(gate_grad.reshape(CAP, sections).T[:, :, None], ((0, 0), (0, 0), (0, tail - 1)))
-    back = exchange(jnp.concatenate([d_input, extra], axis=2))
-    mine = jnp.dot(
-        placing, back.reshape(slots, width + tail), preferred_element_type=jnp.float32
-    ).astype(jnp.bfloat16)
-    return (mine[:, :width].reshape(owned, side, side, feat), mine[:, width])
+    returned = -(-(tokens + 1) // 8) * 8
+    limit = pltpu.CompilerParams(vmem_limit_bytes=24 << 20)
+    back = pl.pallas_call(
+        merge_kernel,
+        out_shape=jax.ShapeDtypeStruct((sections, returned, CAP * feat), jnp.bfloat16),
+        in_specs=vmem(2),
+        out_specs=vmem(1)[0],
+        compiler_params=limit,
+        name="merge",
+    )(near_by(parts), d_input)
+    back = exchange(back)
+    mine, mine_gate = pl.pallas_call(
+        finish_kernel,
+        out_shape=(
+            jax.ShapeDtypeStruct((tokens, owned, feat), jnp.bfloat16),
+            jax.ShapeDtypeStruct((1, owned), jnp.bfloat16),
+        ),
+        in_specs=vmem(2),
+        out_specs=tuple(vmem(2)),
+        compiler_params=limit,
+        name="finish",
+    )(expert_id.reshape(1, owned), near_by(back))
+    mine = mine.reshape(side, side, owned, feat).transpose(2, 0, 1, 3)
+    return (mine, mine_gate.reshape(owned))
 
 
 def solution(mesh):

time: 154 us -> 153 us (level)
  blocking collectives: 68.5 us -> 87.5 us
  starting transfers between devices: 42.6 us -> 30.8 us
  waiting for transfers between devices: 29.3 us -> 22.4 us
  local copies, waits for them, and re-layouts: 2.91 us -> 0.21 us
    all_to_all x1 -> x2, blocking collectives: 26 us -> 45.1 us  [exchange(): lax.all_to_all(array, 'expert', split_axis=0, concat_axis=0, tiled=True)]
    all_to_all x1 -> x0, starting transfers between devices: 11.8 us -> none  [exchange(): lax.all_to_all(array, 'expert', split_axis=0, concat_axis=0, tiled=True)]
    all_to_all x1 -> x0, waiting for transfers between devices: 7.41 us -> none  [exchange(): lax.all_to_all(array, 'expert', split_axis=0, concat_axis=0, tiled=True)]
  transfers between devices with their start and end apart: 8 -> 7, of which waited for: 4 -> 3; matrix products, arithmetic and copies ran while one was open for 0% -> 0% of each run, Pallas kernels for 3% -> 3%
where the time goes in v7:
time: 153 us; the launch traced here: 152 us
  blocking collectives  87.5 us (57%)
  starting transfers between devices  30.8 us (20%)
  waiting for transfers between devices  22.4 us (15%)
  Pallas kernels  10.2 us (7%)
    all_to_all x2, blocking collectives, exchange(): lax.all_to_all(array, 'expert', split_axis=0, concat_axis=0, tiled=True)  45.1 us
    all_gather x1, blocking collectives, on_device(): own = lax.all_gather(packed, 'chan', axis=0, axis_index_groups=families)  42.5 us
    all_to_all x1, waiting for transfers between devices, on_device(): lax.all_to_all(part, 'chan', split_axis=0, concat_axis=0, tiled=True)  19.8 us
    ppermute x6, starting transfers between devices, shift(): lax.ppermute(array, 'chan', [(c, (c + by) % chans) for c in range(chans)])  18.9 us
    all_to_all x1, starting transfers between devices, on_device(): lax.all_to_all(part, 'chan', split_axis=0, concat_axis=0, tiled=True)  11.9 us
  transfers between devices with their start and end apart: 7, of which 3 were waited for; matrix products, arithmetic and copies ran while one was open for 0% of the time, Pallas kernels for 3%

profile of v7, /device:TPU:1, one launch (start us, length us, event | category | flops | bytes accessed | tf_op | source)
XLA Modules:
  0.0 152.1 jit_solution(2320269086207641619)
XLA Ops:
  0.6 0.0 copy-start.3
  0.6 2.1 %prep.1 = bf16[32,24,128]{2,1,0:T(8,128)(2,1)} custom-call(s32[1,32]{1,0:T(1,128)} %bitcast.23, bf16[1,32]{1,0:T(2,128)(2,1)} %bitcast.27, bf16[9,32,64]{2,1,0:T(8,128)(2,1)} %bitcast.25, bf16[9,32,64]{2,1,0:T(8,128)(2,1)} %bitcast.26), custom_call_target="tpu_custom_call" | custom-call | tf_op jit(solution)/shard_map/prep/pallas_call | solution.py:291
  2.7 26.0 %all_to_all.15.in_ref = bf16[32,24,128]{2,1,0:T(8,128)(2,1)S(1)} all-to-all(bf16[32,24,128]{2,1,0:T(8,128)(2,1)} %prep.1), channel_id=1, replica_groups=mesh['expert'=32,'chan'=32] {'expert'}, dimensions={0} | all-to-all | bytes 393216 | tf_op jit(solution)/shard_map/all_to_all | solution.py:288
  28.8 0.2 sort.1
  28.9 42.5 %all-gather = bf16[2304,128]{1,0:T(8,128)(2,1)S(1)} all-gather(bf16[288,128]{1,0:T(8,128)(2,1)S(1)} %get-tuple-element.15), channel_id=2, replica_groups={{0,4,8,12,16,20,24,28},{1,5,9,13,17,21,25,29},{2,6,10,14,18,22,26,30},{..., dimensions={0}, use_global_device_ids=true | all-gather | bytes 663552 | tf_op jit(solution)/shard_map/all_gather | solution.py:319
  71.4 0.0 copy-start.1
  71.4 2.4 %collective-permute-start = (bf16[4,288,128]{2,1,0:T(8,128)(2,1)S(1)}, bf16[4,288,128]{2,1,0:T(8,128)(2,1)S(1)}, u32[]{:S(2)}, u32[]{:S(2)}) collective-permute-start(bf16[4,288,128]{2,1,0:T(8,128)(2,1)S(1)} %get-tuple-element.16.own_low), channel_id=1, source_target_pairs={{0,1},{1,2},{2,3},{3,4},{4,5},{5,6},{6,7},{7,8},{8,9},{9,10},{10,1... | collective-permute-start | bytes 884744 | tf_op jit(solution)/shard_map/ppermute | solution.py:322
  73.8 4.7 %collective-permute-start.2 = (bf16[4,288,128]{2,1,0:T(8,128)(2,1)S(1)}, bf16[4,288,128]{2,1,0:T(8,128)(2,1)S(1)}, u32[]{:S(2)}, u32[]{:S(2)}) collective-permute-start(bf16[4,288,128]{2,1,0:T(8,128)(2,1)S(1)} %get-tuple-element.17.own_high), channel_id=1, source_target_pairs={{0,31},{1,0},{2,1},{3,2},{4,3},{5,4},{6,5},{7,6},{8,7},{9,8},{10,9... | collective-permute-start | bytes 884744 | tf_op jit(solution)/shard_map/ppermute | solution.py:322
  78.6 3.4 %collective-permute-start.4 = (bf16[4,288,128]{2,1,0:T(8,128)(2,1)S(1)}, bf16[4,288,128]{2,1,0:T(8,128)(2,1)S(1)}, u32[]{:S(2)}, u32[]{:S(2)}) collective-permute-start(bf16[4,288,128]{2,1,0:T(8,128)(2,1)S(1)} %get-tuple-element.16.own_low), channel_id=1, source_target_pairs={{0,31},{1,0},{2,1},{3,2},{4,3},{5,4},{6,5},{7,6},{8,7},{9,8},{10,9... | collective-permute-start | bytes 884744 | tf_op jit(solution)/shard_map/ppermute | solution.py:322
  82.0 1.9 %collective-permute-start.5 = (bf16[4,288,128]{2,1,0:T(8,128)(2,1)S(1)}, bf16[4,288,128]{2,1,0:T(8,128)(2,1)S(1)}, u32[]{:S(2)}, u32[]{:S(2)}) collective-permute-start(bf16[4,288,128]{2,1,0:T(8,128)(2,1)S(1)} %get-tuple-element.17.own_high), channel_id=1, source_target_pairs={{0,1},{1,2},{2,3},{3,4},{4,5},{5,6},{6,7},{7,8},{8,9},{9,10},{10,1... | collective-permute-start | bytes 884744 | tf_op jit(solution)/shard_map/ppermute | solution.py:322
  83.9 0.0 collective-permute-done.prev_low
  83.9 1.9 %collective-permute-start.1 = (bf16[4,288,128]{2,1,0:T(8,128)(2,1)S(1)}, bf16[4,288,128]{2,1,0:T(8,128)(2,1)S(1)}, u32[]{:S(2)}, u32[]{:S(2)}) collective-permute-start(bf16[4,288,128]{2,1,0:T(8,128)(2,1)S(1)} %collective-permute-done.prev_low), channel_id=1, source_target_pairs={{0,1},{1,2},{2,3},{3,4},{4,5},{5,6},{6,7},{7,8},{8,9},{9,10},{10,1... | collective-permute-start | bytes 884744 | tf_op jit(solution)/shard_map/ppermute | solution.py:322
  85.8 0.0 collective-permute-done.2.next_high
  85.9 4.6 %collective-permute-start.3 = (bf16[4,288,128]{2,1,0:T(8,128)(2,1)S(1)}, bf16[4,288,128]{2,1,0:T(8,128)(2,1)S(1)}, u32[]{:S(2)}, u32[]{:S(2)}) collective-permute-start(bf16[4,288,128]{2,1,0:T(8,128)(2,1)S(1)} %collective-permute-done.2.next_high), channel_id=1, source_target_pairs={{0,31},{1,0},{2,1},{3,2},{4,3},{5,4},{6,5},{7,6},{8,7},{9,8},{10,9... | collective-permute-start | bytes 884744 | tf_op jit(solution)/shard_map/ppermute | solution.py:322
  90.4 0.0 copy-done.3
  90.4 0.0 copy-start
  90.5 0.1 bitcast_select_fusion.1
  90.6 0.0 copy-done.1
  90.6 1.2 forward.1
  91.8 0.0 collective-permute-done.4.next_low
  91.8 0.0 collective-permute-done.5.prev_high
  91.9 0.2 copy-done
  92.0 2.2 %early.1 = (f32[576,512]{1,0:T(8,128)S(1)}, bf16[512,512]{1,0:T(8,128)(2,1)S(1)}) custom-call(s32[1]{0:T(128)} %bitcast.7.turn_ref, bf16[4,288,128]{2,1,0:T(8,128)(2,1)S(1)} %get-tuple-element.16.own_low, bf16[4,288,128]{2,1,0:T(8,128)(2,1)S(1)} %get-tuple-element.17.own_high, bf16[4,288,128]{2,1,0:T(8,128)(2,1)S(1)} %collective-permute-done.4.next_low, ...), custom_call_target="tpu_custom_call" | custom-call | tf_op jit(solution)/shard_map/early/pallas_call | solution.py:363
  94.2 0.4 collective-permute-done.1.low_ref
  94.6 2.2 %collective-permute-done.3.high_ref = bf16[4,288,128]{2,1,0:T(8,128)(2,1)S(1)} collective-permute-done((bf16[4,288,128]{2,1,0:T(8,128)(2,1)S(1)}, bf16[4,288,128]{2,1,0:T(8,128)(2,1)S(1)}, u32[]{:S(2)}, u32[]{:S(2)}) %collective-permute-start.3) | collective-permute-done | bytes 294944 | tf_op jit(solution)/shard_map/ppermute | solution.py:322
  96.8 2.0 %project.1 = (bf16[9,64,512]{2,1,0:T(8,128)(2,1)S(1)}, f32[32,1,128]{2,1,0:T(1,128)}) custom-call(bf16[4,288,128]{2,1,0:T(8,128)(2,1)S(1)} %collective-permute-done.1.low_ref, bf16[4,288,128]{2,1,0:T(8,128)(2,1)S(1)} %collective-permute-done.3.high_ref, bf16[512,512]{1,0:T(8,128)(2,1)S(1)} %get-tuple-element.18.late_ref, ...), custom_call_target="tpu_custom_call" | custom-call | tf_op jit(solution)/shard_map/project/pallas_call | solution.py:381
  98.7 11.9 %all-to-all-start.1 = ((f32[32,1,128]{2,1,0:T(1,128)}), f32[32,1,128]{2,1,0:T(1,128)S(1)}, u32[]{:S(2)}, u32[]{:S(2)}) async-start(f32[32,1,128]{2,1,0:T(1,128)} %get-tuple-element.23), calls=%async_computation.1 | async-start | bytes 32768 | tf_op jit(solution)/shard_map/all_to_all | solution.py:407
  110.7 0.0 copy-start.2
  110.7 1.3 back.1.d_in_ref
  112.0 19.8 %all-to-all-done.1.parts_ref = f32[32,1,128]{2,1,0:T(1,128)S(1)} async-done(((f32[32,1,128]{2,1,0:T(1,128)}), f32[32,1,128]{2,1,0:T(1,128)S(1)}, u32[]{:S(2)}, u32[]{:S(2)}) %all-to-all-start.1) | async-done | bytes 16416 | tf_op jit(solution)/shard_map/all_to_all | solution.py:407
  131.9 0.2 merge.1
  132.0 19.0 %all_to_all.16.back_ref = bf16[32,16,128]{2,1,0:T(8,128)(2,1)S(1)} all-to-all(bf16[32,16,128]{2,1,0:T(8,128)(2,1)S(1)} %merge.1), channel_id=1, replica_groups=mesh['expert'=32,'chan'=32] {'expert'}, dimensions={0} | all-to-all | bytes 262144 | tf_op jit(solution)/shard_map/all_to_all | solution.py:288
  151.0 0.0 copy-done.2
  151.0 1.0 finish.1
  (3 shorter events, 0.1 us)
Async XLA Ops:
  0.6 89.8 %copy-start.3 = (bf16[1,3,3,32,512]{4,3,2,1,0:T(8,128)(2,1)S(1)}, bf16[1,3,3,32,512]{4,3,2,1,0:T(8,128)(2,1)}, u32[]{:S(2)}) copy-start(bf16[1,3,3,32,512]{4,3,2,1,0:T(8,128)(2,1)} %param.11) | copy-start | bytes 884740
  71.4 19.2 %copy-start.1 = (bf16[1,9,512]{2,1,0:T(8,128)(2,1)S(1)}, bf16[1,9,512]{2,1,0:T(8,128)(2,1)}, u32[]{:S(2)}) copy-start(bf16[1,9,512]{2,1,0:T(8,128)(2,1)} %param.12) | copy-start | bytes 27652
  71.4 12.5 %collective-permute-start = (bf16[4,288,128]{2,1,0:T(8,128)(2,1)S(1)}, bf16[4,288,128]{2,1,0:T(8,128)(2,1)S(1)}, u32[]{:S(2)}, u32[]{:S(2)}) collective-permute-start(bf16[4,288,128]{2,1,0:T(8,128)(2,1)S(1)} %get-tuple-element.16.own_low), channel_id=1, source_target_pairs={{0,1},{1,2},{2,3},{3,4},{4,5},{5,6},{6,7},{7,8},{8,9},{9,10},{10,1... | collective-permute-start | bytes 884744 | tf_op jit(solution)/shard_map/ppermute | solution.py:322
  73.8 12.0 %collective-permute-start.2 = (bf16[4,288,128]{2,1,0:T(8,128)(2,1)S(1)}, bf16[4,288,128]{2,1,0:T(8,128)(2,1)S(1)}, u32[]{:S(2)}, u32[]{:S(2)}) collective-permute-start(bf16[4,288,128]{2,1,0:T(8,128)(2,1)S(1)} %get-tuple-element.17.own_high), channel_id=1, source_target_pairs={{0,31},{1,0},{2,1},{3,2},{4,3},{5,4},{6,5},{7,6},{8,7},{9,8},{10,9... | collective-permute-start | bytes 884744 | tf_op jit(solution)/shard_map/ppermute | solution.py:322
  78.6 13.2 %collective-permute-start.4 = (bf16[4,288,128]{2,1,0:T(8,128)(2,1)S(1)}, bf16[4,288,128]{2,1,0:T(8,128)(2,1)S(1)}, u32[]{:S(2)}, u32[]{:S(2)}) collective-permute-start(bf16[4,288,128]{2,1,0:T(8,128)(2,1)S(1)} %get-tuple-element.16.own_low), channel_id=1, source_target_pairs={{0,31},{1,0},{2,1},{3,2},{4,3},{5,4},{6,5},{7,6},{8,7},{9,8},{10,9... | collective-permute-start | bytes 884744 | tf_op jit(solution)/shard_map/ppermute | solution.py:322
  82.0 9.9 %collective-permute-start.5 = (bf16[4,288,128]{2,1,0:T(8,128)(2,1)S(1)}, bf16[4,288,128]{2,1,0:T(8,128)(2,1)S(1)}, u32[]{:S(2)}, u32[]{:S(2)}) collective-permute-start(bf16[4,288,128]{2,1,0:T(8,128)(2,1)S(1)} %get-tuple-element.17.own_high), channel_id=1, source_target_pairs={{0,1},{1,2},{2,3},{3,4},{4,5},{5,6},{6,7},{7,8},{8,9},{9,10},{10,1... | collective-permute-start | bytes 884744 | tf_op jit(solution)/shard_map/ppermute | solution.py:322
  83.9 10.7 %collective-permute-start.1 = (bf16[4,288,128]{2,1,0:T(8,128)(2,1)S(1)}, bf16[4,288,128]{2,1,0:T(8,128)(2,1)S(1)}, u32[]{:S(2)}, u32[]{:S(2)}) collective-permute-start(bf16[4,288,128]{2,1,0:T(8,128)(2,1)S(1)} %collective-permute-done.prev_low), channel_id=1, source_target_pairs={{0,1},{1,2},{2,3},{3,4},{4,5},{5,6},{6,7},{7,8},{8,9},{9,10},{10,1... | collective-permute-start | bytes 884744 | tf_op jit(solution)/shard_map/ppermute | solution.py:322
  85.9 10.9 %collective-permute-start.3 = (bf16[4,288,128]{2,1,0:T(8,128)(2,1)S(1)}, bf16[4,288,128]{2,1,0:T(8,128)(2,1)S(1)}, u32[]{:S(2)}, u32[]{:S(2)}) collective-permute-start(bf16[4,288,128]{2,1,0:T(8,128)(2,1)S(1)} %collective-permute-done.2.next_high), channel_id=1, source_target_pairs={{0,31},{1,0},{2,1},{3,2},{4,3},{5,4},{6,5},{7,6},{8,7},{9,8},{10,9... | collective-permute-start | bytes 884744 | tf_op jit(solution)/shard_map/ppermute | solution.py:322
  90.4 1.6 %copy-start = (bf16[1,512,2048]{2,1,0:T(8,128)(2,1)S(1)}, bf16[1,512,2048]{2,1,0:T(8,128)(2,1)}, u32[]{:S(2)}) copy-start(bf16[1,512,2048]{2,1,0:T(8,128)(2,1)} %param.13) | copy-start | bytes 6291460
  98.7 33.1 %all-to-all-start.1 = ((f32[32,1,128]{2,1,0:T(1,128)}), f32[32,1,128]{2,1,0:T(1,128)S(1)}, u32[]{:S(2)}, u32[]{:S(2)}) async-start(f32[32,1,128]{2,1,0:T(1,128)} %get-tuple-element.23), calls=%async_computation.1 | async-start | bytes 32768 | tf_op jit(solution)/shard_map/all_to_all | solution.py:407
  110.7 40.4 %copy-start.2 = (s32[32,1]{0,1:T(1,128)S(1)}, s32[32,1]{0,1:T(1,128)}, u32[]{:S(2)}) copy-start(s32[32,1]{0,1:T(1,128)} %param.10) | copy-start | bytes 388
